TPU v7x, 256 devices: a whole 4x4x8 slice. The times are simulated.
256 devices in a mesh: seq: 128 (over z, y, x), head: 2 (over core).
Axes of the slice: x: 4, y: 4, z: 8, core: 2. Of those that a mesh axis runs over, the one named last changes fastest.
Arguments:
- input_rows: bfloat16 [32768, 4096], P(('seq', 'head')), may hold values from -40 to 40
- doc_lengths: int32 [64], replicated, may hold values from 1 to 1024, 32768 in all
- w_query: bfloat16 [4096, 4096], P(None, 'head'), may hold values from -0.09375 to 0.09375
- key_weight: bfloat16 [4096, 1024], P(None, 'head'), may hold values from -0.09375 to 0.09375
- value_weight: bfloat16 [4096, 1024], P(None, 'head'), may hold values from -0.09375 to 0.09375
- w_out: bfloat16 [4096, 4096], P('head'), may hold values from -0.5 to 0.5
Outputs:
- mixed: bfloat16 [32768, 4096], P(('seq', 'head'))
All inputs are finite; a program needn't handle non-finite values.
Results may differ from a plain program's by a relative error of at most 0.013.
Values may be sent and summed in bfloat16 or wider, within the bound.
A program may use at most 192 MiB of HBM per device.

v0:
```python
import math

import jax
import jax.numpy as jnp
from jax import lax
from jax.sharding import PartitionSpec as P

HEAD_SIZE = 128
REACH = 4


NEG_FILL = -1e30


def passed_along(value, axis, steps):
    count = lax.axis_size(axis)
    first, last = (max(0, -steps), min(count, count - steps))
    return lax.ppermute(value, axis, [(source, source + steps) for source in range(first, last)])


def inverse_frequency():
    table = []
    for number in range(HEAD_SIZE // 2):
        base_freq = 500000.0 ** (-(2.0 * number) / HEAD_SIZE)
        wavelength = 2.0 * math.pi / base_freq
        smooth = (8192.0 / wavelength - 1.0) / 3.0
        if wavelength < 2048.0:
            table.append(base_freq)
        elif wavelength > 8192.0:
            table.append(base_freq / 8.0)
        else:
            table.append((1.0 - smooth) * base_freq / 8.0 + smooth * base_freq)
    return jnp.asarray(table, dtype=jnp.float32)


def rotate(value_matrix, cosine, sine_table):
    half_size = value_matrix.shape[-1] // 2
    first = value_matrix[..., :half_size]
    second = value_matrix[..., half_size:]
    return jnp.concatenate(
        [first * cosine - second * sine_table, second * cosine + first * sine_table], axis=-1
    )


def doc_of(positions, doc_ends):
    return jnp.sum((positions[:, None] >= doc_ends[None, :]).astype(jnp.int32), axis=1)


def body(input_rows, doc_lengths, w_query, key_weight, value_weight, w_out):
    width_q = w_query.shape[1]
    width_k = key_weight.shape[1]
    heads_here = width_q // HEAD_SIZE
    kv_here = width_k // HEAD_SIZE
    query_group = heads_here // kv_here
    piece = lax.all_gather(input_rows, "head", axis=0, tiled=True)
    projected = jnp.concatenate(
        [
            jnp.dot(piece, w_query, preferred_element_type=jnp.float32),
            jnp.dot(piece, key_weight, preferred_element_type=jnp.float32),
            jnp.dot(piece, value_weight, preferred_element_type=jnp.float32),
        ],
        axis=1,
    )
    tok_seq = projected.shape[0]
    seq_index = lax.axis_index("seq")
    positions = seq_index * tok_seq + jnp.arange(tok_seq, dtype=jnp.int32)
    doc_ends = jnp.cumsum(doc_lengths)
    query_docs = doc_of(positions, doc_ends)
    angles = positions.astype(jnp.float32)[:, None] * inverse_frequency()[None, :]
    cosine = jnp.cos(angles)[:, None, :]
    sine_table = jnp.sin(angles)[:, None, :]
    query_matrix = rotate(
        projected[:, :width_q].reshape(tok_seq, heads_here, HEAD_SIZE), cosine, sine_table
    )
    query_matrix = query_matrix.astype(jnp.bfloat16).reshape(
        tok_seq, kv_here, query_group, HEAD_SIZE
    )
    key_matrix = rotate(
        projected[:, width_q : width_q + width_k].reshape(tok_seq, kv_here, HEAD_SIZE),
        cosine,
        sine_table,
    )
    key_matrix = key_matrix.astype(jnp.bfloat16).reshape(tok_seq, width_k)
    value_matrix = projected[:, width_q + width_k :].astype(jnp.bfloat16)
    scale = HEAD_SIZE ** (-0.5)

    def attend(state, key_rows, value_rows, key_pos):
        running_max, running_sum, weighted = state
        count = key_rows.shape[0]
        key_block = key_rows.reshape(count, kv_here, HEAD_SIZE)
        value_block = value_rows.reshape(count, kv_here, HEAD_SIZE)
        key_docs = doc_of(key_pos, doc_ends)
        scores = (
            jnp.einsum(
                "tkgd,skd->kgts", query_matrix, key_block, preferred_element_type=jnp.float32
            )
            * scale
        )
        allowed = (
            (query_docs[:, None] == key_docs[None, :])
            & (key_pos[None, :] <= positions[:, None])
            & (key_pos[None, :] >= 0)
        )
        scores = jnp.where(allowed, scores, NEG_FILL)
        new_max = jnp.maximum(running_max, jnp.max(scores, axis=-1))
        factor = jnp.exp(running_max - new_max)
        weights = jnp.where(allowed, jnp.exp(scores - new_max[..., None]), 0.0)
        running_sum = running_sum * factor + jnp.sum(weights, axis=-1)
        weighted = weighted * factor[..., None] + jnp.einsum(
            "kgts,skd->kgtd",
            weights.astype(jnp.bfloat16),
            value_block,
            preferred_element_type=jnp.float32,
        )
        return (new_max, running_sum, weighted)

    initial = (
        jnp.full((kv_here, query_group, tok_seq), NEG_FILL, jnp.float32),
        jnp.zeros((kv_here, query_group, tok_seq), jnp.float32),
        jnp.zeros((kv_here, query_group, tok_seq, HEAD_SIZE), jnp.float32),
    )
    state = attend(initial, key_matrix, value_matrix, positions)
    for distance in range(1, REACH + 1):
        earlier = passed_along((key_matrix, value_matrix), "seq", distance)
        state = attend(state, earlier[0], earlier[1], positions - distance * tok_seq)
    final_max, final_sum, final_weighted = state
    attended = (final_weighted / final_sum[..., None]).transpose(2, 0, 1, 3)
    attended = attended.reshape(tok_seq, heads_here * HEAD_SIZE).astype(jnp.bfloat16)
    return lax.psum_scatter(
        jnp.dot(attended, w_out, preferred_element_type=jnp.float32).astype(jnp.bfloat16),
        "head",
        scatter_dimension=0,
        tiled=True,
    )


def solution(mesh):
    in_specs = (
        P(("seq", "head"), None),
        P(),
        P(None, "head"),
        P(None, "head"),
        P(None, "head"),
        P("head", None),
    )
    out_specs = P(("seq", "head"), None)
    return jax.shard_map(body, mesh=mesh, in_specs=in_specs, out_specs=out_specs, check_vma=False)
```

profile of v0, /device:TPU:1, one launch (start us, length us, event | category | flops | bytes accessed | tf_op | source)
XLA Modules:
  0.0 153.8 jit_solution(9673739192024044991)
XLA Ops:
  6.5 0.7 all-gather.2.cloned.1.call-update
  7.3 0.7 copy.43
  8.5 1.2 multiply_cosine_fusion
  9.7 0.7 and_and_fusion.4
  10.4 19.2 %all-gather.2.cloned.1.call-done = bf16[256,4096]{1,0:T(8,128)(2,1)} async-done(((bf16[128,4096]{1,0:T(8,128)(2,1)}), bf16[256,4096]{1,0:T(8,128)(2,1)}) %all-gather.2.cloned.1.call-update) | async-done | bytes 2097168 | tf_op jit(solution)/shard_map/all_gather | solution.py:55
  29.6 4.1 %fusion.94 = f32[256,512]{1,0:T(8,128)S(1)} fusion(bf16[256,4096]{1,0:T(8,128)(2,1)} %all-gather.2.cloned.1.call-done, bf16[4096,512]{1,0:T(8,128)(2,1)} %param.10), kind=kOutput, calls=%fused_computation.140 | convolution fusion | flops 1073741824 | bytes 6815744 | tf_op jit(solution)/shard_map/dot_general | solution.py:59
  33.7 0.2 reshape.280
  33.9 0.3 fusion.93
  34.2 0.1 multiply_subtract_fusion
  34.4 0.1 maximum_convert_fusion
  34.5 0.1 copy.50
  34.7 4.4 %collective-permute-start.2 = (bf16[256,512]{0,1:T(8,128)(2,1)S(1)}, bf16[256,512]{0,1:T(8,128)(2,1)S(1)}, u32[]{:S(2)}, u32[]{:S(2)}) collective-permute-start(bf16[256,512]{0,1:T(8,128)(2,1)S(1)} %bitcast.274), channel_id=1, source_target_pairs={{0,4},{2,6},{4,8},{6,10},{8,12},{10,14},{12,16},{14,18},{16,20},{1... | collective-permute-start | bytes 786440 | tf_op jit(solution)/shard_map/ppermute | solution.py:18
  39.0 2.2 %collective-permute-start = (bf16[256,512]{0,1:T(8,128)(2,1)S(1)}, bf16[256,512]{0,1:T(8,128)(2,1)S(1)}, u32[]{:S(2)}, u32[]{:S(2)}) collective-permute-start(bf16[256,512]{0,1:T(8,128)(2,1)S(1)} %bitcast.275), channel_id=1, source_target_pairs={{0,2},{2,4},{4,6},{6,8},{8,10},{10,12},{12,14},{14,16},{16,18},{18... | collective-permute-start | bytes 786440 | tf_op jit(solution)/shard_map/ppermute | solution.py:18
  41.3 3.1 %collective-permute-start.6 = (bf16[256,512]{0,1:T(8,128)(2,1)S(1)}, bf16[256,512]{0,1:T(8,128)(2,1)S(1)}, u32[]{:S(2)}, u32[]{:S(2)}) collective-permute-start(bf16[256,512]{0,1:T(8,128)(2,1)S(1)} %bitcast.276), channel_id=1, source_target_pairs={{0,8},{2,10},{4,12},{6,14},{8,16},{10,18},{12,20},{14,22},{16,24},... | collective-permute-start | bytes 786440 | tf_op jit(solution)/shard_map/ppermute | solution.py:18
  44.4 5.2 %collective-permute-start.4 = (bf16[256,512]{0,1:T(8,128)(2,1)S(1)}, bf16[256,512]{0,1:T(8,128)(2,1)S(1)}, u32[]{:S(2)}, u32[]{:S(2)}) collective-permute-start(bf16[256,512]{0,1:T(8,128)(2,1)S(1)} %bitcast.277), channel_id=1, source_target_pairs={{0,6},{2,8},{4,10},{6,12},{8,14},{10,16},{12,18},{14,20},{16,22},{... | collective-permute-start | bytes 786440 | tf_op jit(solution)/shard_map/ppermute | solution.py:18
  49.6 4.1 %convolution_convert_fusion.1 = bf16[256,512]{1,0:T(8,128)(2,1)S(1)} fusion(bf16[256,4096]{1,0:T(8,128)(2,1)} %all-gather.2.cloned.1.call-done, bf16[4096,512]{1,0:T(8,128)(2,1)} %param.11), kind=kOutput, calls=%fused_computation.70 | convolution fusion | flops 1073872896 | bytes 6553600 | tf_op jit(solution)/shard_map/dot_general | solution.py:60
  53.7 0.1 copy.78
  53.8 1.3 collective-permute-start.1
  55.1 8.7 %convolution_bitcast_fusion = f32[32,8,16,128]{3,1,2,0:T(8,128)S(1)} fusion(bf16[256,4096]{1,0:T(8,128)(2,1)} %all-gather.2.cloned.1.call-done, bf16[4096,2048]{1,0:T(8,128)(2,1)} %param.9), kind=kOutput, calls=%fused_computation.69 | convolution fusion | flops 4294967296 | bytes 20971520 | tf_op jit(solution)/shard_map/dot_general | solution.py:58
  63.9 0.4 copy.93
  64.3 0.8 subtract_convert_fusion
  65.0 0.3 copy.46
  65.3 0.3 copy.47
  65.6 0.6 pad_maximum_fusion
  66.2 0.8 fusion
  67.0 4.0 %collective-permute-start.3 = (bf16[256,512]{1,0:T(8,128)(2,1)S(1)}, bf16[256,512]{1,0:T(8,128)(2,1)S(1)}, u32[]{:S(2)}, u32[]{:S(2)}) collective-permute-start(bf16[256,512]{1,0:T(8,128)(2,1)S(1)} %convolution_convert_fusion.1), channel_id=1, source_target_pairs={{0,4},{2,6},{4,8},{6,10},{8,12},{10,14},{12,16},{14,18},{16,20},{1... | collective-permute-start | bytes 786440 | tf_op jit(solution)/shard_map/ppermute | solution.py:18
  71.0 2.9 %fusion.2 = (f32[4,4,256]{2,1,0:T(4,128)S(1)}, f32[4,256,256,4]{2,1,3,0:T(8,128)}) fusion(pred[256,256]{0,1:T(8,128)(4,1)S(1)} %get-tuple-element.28, bf16[256,4,128,1]{0,2,3,1:T(8,128)(2,1)S(1)} %bitcast.272, bf16[256,4,4,128]{3,0,2,1:T(8,128)(2,1)S(1)} %pad_maximum_fusion), kind=kOutput, calls=%fused_computation.13 | convolution fusion | flops 271577088 | bytes 5586944 | tf_op jit(solution)/shard_map/tkgd,skd->kgts/dot_general | solution.py:94
  73.8 3.7 %collective-permute-start.5 = (bf16[256,512]{1,0:T(8,128)(2,1)S(1)}, bf16[256,512]{1,0:T(8,128)(2,1)S(1)}, u32[]{:S(2)}, u32[]{:S(2)}) collective-permute-start(bf16[256,512]{1,0:T(8,128)(2,1)S(1)} %convolution_convert_fusion.1), channel_id=1, source_target_pairs={{0,6},{2,8},{4,10},{6,12},{8,14},{10,16},{12,18},{14,20},{16,22},{... | collective-permute-start | bytes 786440 | tf_op jit(solution)/shard_map/ppermute | solution.py:18
  77.6 0.9 fusion.1
  78.5 3.3 %collective-permute-start.7 = (bf16[256,512]{1,0:T(8,128)(2,1)S(1)}, bf16[256,512]{1,0:T(8,128)(2,1)S(1)}, u32[]{:S(2)}, u32[]{:S(2)}) collective-permute-start(bf16[256,512]{1,0:T(8,128)(2,1)S(1)} %convolution_convert_fusion.1), channel_id=1, source_target_pairs={{0,8},{2,10},{4,12},{6,14},{8,16},{10,18},{12,20},{14,22},{16,24},... | collective-permute-start | bytes 786440 | tf_op jit(solution)/shard_map/ppermute | solution.py:18
  81.8 2.8 %fusion.4 = (f32[4,4,256]{2,1,0:T(4,128)S(1)}, f32[4,256,256,4]{2,1,3,0:T(8,128)}) fusion(pred[256,256]{0,1:T(8,128)(4,1)S(1)} %get-tuple-element.30, bf16[256,4,128,1]{0,2,3,1:T(8,128)(2,1)S(1)} %bitcast.270, bf16[256,4,4,128]{3,0,2,1:T(8,128)(2,1)S(1)} %pad_maximum_fusion), kind=kOutput, calls=%fused_computation.15 | convolution fusion | flops 271577088 | bytes 5586944 | tf_op jit(solution)/shard_map/tkgd,skd->kgts/dot_general | solution.py:94
  84.6 2.9 %fusion.3 = (f32[4,4,256]{2,1,0:T(4,128)S(1)}, f32[4,256,256,4]{2,1,3,0:T(8,128)}) fusion(pred[256,256]{0,1:T(8,128)(4,1)S(1)} %get-tuple-element.29, bf16[256,4,128,1]{0,2,3,1:T(8,128)(2,1)S(1)} %bitcast.269, bf16[256,4,4,128]{3,0,2,1:T(8,128)(2,1)S(1)} %pad_maximum_fusion), kind=kOutput, calls=%fused_computation.14 | convolution fusion | flops 271577088 | bytes 5586944 | tf_op jit(solution)/shard_map/tkgd,skd->kgts/dot_general | solution.py:94
  87.5 1.0 fusion.5
  88.5 2.5 %fusion.23 = f32[4,4,256,128]{2,3,1,0:T(8,128)} fusion(bf16[256,4,128,1]{0,2,3,1:T(8,128)(2,1)S(1)} %bitcast.273, f32[4,256,256,4]{2,1,3,0:T(8,128)S(1)} %get-tuple-element.43, f32[4,4,256]{2,1,0:T(4,128)S(1)} %get-tuple-element.26, pred[256,256]{0,1:T(8,128)(4,1)S(1)} %get-tuple-element.27), kind=kOutput, calls=%fused_computation.30 | convolution fusion | flops 273678336 | bytes 6635520 | tf_op jit(solution)/shard_map/kgts,skd->kgtd/dot_general | solution.py:109
  91.1 1.0 fusion.7
  92.1 0.1 copy.81
  92.3 4.9 %fusion.21 = f32[4,4,256,128]{2,3,1,0:T(8,128)} fusion(bf16[256,4,128,1]{0,2,3,1:T(8,128)(2,1)S(1)} %bitcast.279, f32[4,256,256,4]{2,1,3,0:T(8,128)} %copy-done.3, f32[4,4,256]{2,1,0:T(4,128)S(1)} %get-tuple-element.17, pred[256,256]{0,1:T(8,128)(4,1)S(1)} %get-tuple-element.31), kind=kOutput, calls=%fused_computation.29 | convolution fusion | flops 273678336 | bytes 6635520 | tf_op jit(solution)/shard_map/kgts,skd->kgtd/dot_general | solution.py:109
  97.2 1.0 fusion.9
  98.2 0.1 copy.84
  98.4 4.9 %fusion.19 = f32[4,4,256,128]{2,3,1,0:T(8,128)} fusion(bf16[256,4,128,1]{0,2,3,1:T(8,128)(2,1)S(1)} %bitcast.280, f32[4,256,256,4]{2,1,3,0:T(8,128)} %get-tuple-element.39, f32[4,4,256]{2,1,0:T(4,128)S(1)} %get-tuple-element.16, pred[256,256]{0,1:T(8,128)(4,1)S(1)} %get-tuple-element.28), kind=kOutput, calls=%fused_computation.28 | convolution fusion | flops 273678336 | bytes 6635520 | tf_op jit(solution)/shard_map/kgts,skd->kgtd/dot_general | solution.py:109
  103.3 1.0 fusion.11
  104.3 0.1 copy.87
  104.5 4.9 %fusion.17 = f32[4,4,256,128]{2,3,1,0:T(8,128)} fusion(bf16[256,4,128,1]{0,2,3,1:T(8,128)(2,1)S(1)} %bitcast.281, f32[4,256,256,4]{2,1,3,0:T(8,128)} %get-tuple-element.37, f32[4,4,256]{2,1,0:T(4,128)S(1)} %get-tuple-element.15, pred[256,256]{0,1:T(8,128)(4,1)S(1)} %get-tuple-element.29), kind=kOutput, calls=%fused_computation.27 | convolution fusion | flops 273678336 | bytes 6635520 | tf_op jit(solution)/shard_map/kgts,skd->kgtd/dot_general | solution.py:109
  109.3 1.0 fusion.13
  110.4 0.1 copy.90
  110.6 6.6 %fusion.26 = bf16[256,4,4,128]{0,3,2,1:T(8,128)(2,1)S(1)} fusion(f32[4,4,256,128]{2,3,1,0:T(8,128)} %fusion.17, f32[4,4,256,128]{2,3,1,0:T(8,128)} %fusion.19, f32[4,4,256,128]{2,3,1,0:T(8,128)} %fusion.21, f32[4,4,256,128]{2,3,1,0:T(8,128)} %fusion.23, f32[256,4,4]{0,2,1:T(4,128)S(1)} %get-tuple-element.10, f32[256,4,4]{0,2,1:T(4,128)S(1)} %get-tuple-element.13, ...), kind=kOutput, calls=%fused_computation.33 | convolution fusion | flops 279445504 | bytes 14073856 | tf_op jit(solution)/shard_map/kgts,skd->kgtd/dot_general | solution.py:109
  117.2 11.6 %convolution_convert_fusion = bf16[256,4096]{1,0:T(8,128)(2,1)} fusion(bf16[256,2048]{0,1:T(8,128)(2,1)S(1)} %bitcast.268, bf16[2048,4096]{1,0:T(8,128)(2,1)} %param.12), kind=kOutput, calls=%fused_computation | convolution fusion | flops 4296015872 | bytes 19922944 | tf_op jit(solution)/shard_map/dot_general | solution.py:130
  128.8 18.1 %reduce-scatter.2.cloned.1.call-done = bf16[128,4096]{1,0:T(8,128)(2,1)} async-done(((bf16[256,4096]{1,0:T(8,128)(2,1)}), bf16[128,4096]{1,0:T(8,128)(2,1)}) %reduce-scatter.2.cloned.1.call-update) | async-done | bytes 1048592 | tf_op jit(solution)/shard_map/reduce_scatter | solution.py:129
  (30 shorter events, 0.5 us)
Async XLA Ops:
  6.5 23.1 %all-gather.2.cloned.1.call-start = ((), (), s32[]{:S(2)}) async-start(), calls=%async_computation.1 | async-start | bytes 3145728 | tf_op jit(solution)/shard_map/all_gather | solution.py:55
  7.3 139.7 %reduce-scatter.2.cloned.1.call-start = ((), (), s32[]{:S(2)}) async-start(), calls=%async_computation.2 | async-start | bytes 3145728 | tf_op jit(solution)/shard_map/reduce_scatter | solution.py:129
  34.7 32.3 %collective-permute-start.2 = (bf16[256,512]{0,1:T(8,128)(2,1)S(1)}, bf16[256,512]{0,1:T(8,128)(2,1)S(1)}, u32[]{:S(2)}, u32[]{:S(2)}) collective-permute-start(bf16[256,512]{0,1:T(8,128)(2,1)S(1)} %bitcast.274), channel_id=1, source_target_pairs={{0,4},{2,6},{4,8},{6,10},{8,12},{10,14},{12,16},{14,18},{16,20},{1... | collective-permute-start | bytes 786440 | tf_op jit(solution)/shard_map/ppermute | solution.py:18
  39.0 34.8 %collective-permute-start = (bf16[256,512]{0,1:T(8,128)(2,1)S(1)}, bf16[256,512]{0,1:T(8,128)(2,1)S(1)}, u32[]{:S(2)}, u32[]{:S(2)}) collective-permute-start(bf16[256,512]{0,1:T(8,128)(2,1)S(1)} %bitcast.275), channel_id=1, source_target_pairs={{0,2},{2,4},{4,6},{6,8},{8,10},{10,12},{12,14},{14,16},{16,18},{18... | collective-permute-start | bytes 786440 | tf_op jit(solution)/shard_map/ppermute | solution.py:18
  41.3 37.2 %collective-permute-start.6 = (bf16[256,512]{0,1:T(8,128)(2,1)S(1)}, bf16[256,512]{0,1:T(8,128)(2,1)S(1)}, u32[]{:S(2)}, u32[]{:S(2)}) collective-permute-start(bf16[256,512]{0,1:T(8,128)(2,1)S(1)} %bitcast.276), channel_id=1, source_target_pairs={{0,8},{2,10},{4,12},{6,14},{8,16},{10,18},{12,20},{14,22},{16,24},... | collective-permute-start | bytes 786440 | tf_op jit(solution)/shard_map/ppermute | solution.py:18
  44.4 40.2 %collective-permute-start.4 = (bf16[256,512]{0,1:T(8,128)(2,1)S(1)}, bf16[256,512]{0,1:T(8,128)(2,1)S(1)}, u32[]{:S(2)}, u32[]{:S(2)}) collective-permute-start(bf16[256,512]{0,1:T(8,128)(2,1)S(1)} %bitcast.277), channel_id=1, source_target_pairs={{0,6},{2,8},{4,10},{6,12},{8,14},{10,16},{12,18},{14,20},{16,22},{... | collective-permute-start | bytes 786440 | tf_op jit(solution)/shard_map/ppermute | solution.py:18
  53.8 38.3 %collective-permute-start.1 = (bf16[256,512]{1,0:T(8,128)(2,1)S(1)}, bf16[256,512]{1,0:T(8,128)(2,1)S(1)}, u32[]{:S(2)}, u32[]{:S(2)}) collective-permute-start(bf16[256,512]{1,0:T(8,128)(2,1)S(1)} %convolution_convert_fusion.1), channel_id=1, source_target_pairs={{0,2},{2,4},{4,6},{6,8},{8,10},{10,12},{12,14},{14,16},{16,18},{18... | collective-permute-start | bytes 786440 | tf_op jit(solution)/shard_map/ppermute | solution.py:18
  67.0 31.2 %collective-permute-start.3 = (bf16[256,512]{1,0:T(8,128)(2,1)S(1)}, bf16[256,512]{1,0:T(8,128)(2,1)S(1)}, u32[]{:S(2)}, u32[]{:S(2)}) collective-permute-start(bf16[256,512]{1,0:T(8,128)(2,1)S(1)} %convolution_convert_fusion.1), channel_id=1, source_target_pairs={{0,4},{2,6},{4,8},{6,10},{8,12},{10,14},{12,16},{14,18},{16,20},{1... | collective-permute-start | bytes 786440 | tf_op jit(solution)/shard_map/ppermute | solution.py:18
  73.8 30.5 %collective-permute-start.5 = (bf16[256,512]{1,0:T(8,128)(2,1)S(1)}, bf16[256,512]{1,0:T(8,128)(2,1)S(1)}, u32[]{:S(2)}, u32[]{:S(2)}) collective-permute-start(bf16[256,512]{1,0:T(8,128)(2,1)S(1)} %convolution_convert_fusion.1), channel_id=1, source_target_pairs={{0,6},{2,8},{4,10},{6,12},{8,14},{10,16},{12,18},{14,20},{16,22},{... | collective-permute-start | bytes 786440 | tf_op jit(solution)/shard_map/ppermute | solution.py:18
  78.5 12.6 %copy-start.3 = (f32[4,256,256,4]{2,1,3,0:T(8,128)}, f32[4,256,256,4]{2,1,3,0:T(8,128)S(1)}, u32[]{:S(2)}) copy-start(f32[4,256,256,4]{2,1,3,0:T(8,128)S(1)} %get-tuple-element.41) | copy-start | bytes 12582916
  78.5 31.9 %collective-permute-start.7 = (bf16[256,512]{1,0:T(8,128)(2,1)S(1)}, bf16[256,512]{1,0:T(8,128)(2,1)S(1)}, u32[]{:S(2)}, u32[]{:S(2)}) collective-permute-start(bf16[256,512]{1,0:T(8,128)(2,1)S(1)} %convolution_convert_fusion.1), channel_id=1, source_target_pairs={{0,8},{2,10},{4,12},{6,14},{8,16},{10,18},{12,20},{14,22},{16,24},... | collective-permute-start | bytes 786440 | tf_op jit(solution)/shard_map/ppermute | solution.py:18
  92.3 4.9 %copy-start.1 = (f32[4,256,256,4]{2,1,3,0:T(8,128)S(1)}, f32[4,256,256,4]{2,1,3,0:T(8,128)}, u32[]{:S(2)}) copy-start(f32[4,256,256,4]{2,1,3,0:T(8,128)} %get-tuple-element.39) | copy-start | bytes 12582916
  98.4 4.9 %copy-start.2 = (f32[4,256,256,4]{2,1,3,0:T(8,128)S(1)}, f32[4,256,256,4]{2,1,3,0:T(8,128)}, u32[]{:S(2)}) copy-start(f32[4,256,256,4]{2,1,3,0:T(8,128)} %get-tuple-element.37) | copy-start | bytes 12582916
  104.5 4.9 %copy-start = (f32[4,256,256,4]{2,1,3,0:T(8,128)S(1)}, f32[4,256,256,4]{2,1,3,0:T(8,128)}, u32[]{:S(2)}) copy-start(f32[4,256,256,4]{2,1,3,0:T(8,128)} %get-tuple-element.35) | copy-start | bytes 12582916
Sparse Core Ops, SparseCore 0:
  9.2 20.4 all-gather.1
  128.9 17.9 reduce-scatter.1
where the time goes:
time: 154 us
  matrix products  62.4 us (41%)
  waiting for transfers between devices  38.1 us (25%)
  starting transfers between devices  27.3 us (18%)
  between operations  13.8 us (9%)
  other arithmetic  9.22 us (6%)
  local copies, waits for them, and re-layouts  3.01 us (2%)
    ppermute x8, starting transfers between devices, passed_along(): lax.ppermute(value, axis, [(source, source + steps) for source in range(f...  27.2 us
    dot_general x5, matrix products, attend(): jnp.einsum('kgts,skd->kgtd', weights.astype(jnp.bfloat16), value_block, p...  23.8 us
    all_gather x1, waiting for transfers between devices, body(): piece = lax.all_gather(input_rows, 'head', axis=0, tiled=True)  19.2 us
    reduce_scatter x1, waiting for transfers between devices, body(): lax.psum_scatter(jnp.dot(attended, w_out, preferred_element_type=jnp.floa...  18.1 us
    dot_general x1, matrix products, body(): jnp.dot(attended, w_out, preferred_element_type=jnp.float32)  11.6 us
    dot_general x5, matrix products, attend(): jnp.einsum('tkgd,skd->kgts', query_matrix, key_block, preferred_element_t...  10.2 us
    dot_general x1, matrix products, body(): jnp.dot(piece, w_query, preferred_element_type=jnp.float32)  8.73 us
    reduce_sum x5, other arithmetic, attend(): running_sum = running_sum * factor + jnp.sum(weights, axis=-1)  5.24 us
  transfers between devices with their start and end apart: 10, of which 2 were waited for; matrix products, arithmetic and copies ran while one was open for 33% of the time, Pallas kernels for 0%

commit v1 on v0

v1 whole, which is shorter than its diff:
```python
import math

import jax
import jax.numpy as jnp
import numpy as np
from jax import lax
from jax.experimental import pallas as pl
from jax.experimental.pallas import tpu as pltpu
from jax.sharding import PartitionSpec as P

MESH = pl.DeviceIdType.MESH
HEAD_SIZE = 128
TOK = 256
HALF = 128
WIDTH = 4096
KV_HERE = 4
GROUP = 4
SLOTS = 5
X_RING = 4
N_SEQ = 128
DOCS = 64
NEG_FILL = -1e30
COLS = 512
CHUNKS = WIDTH // COLS

TO_Y, TO_RIGHT, TO_LEFT, ON_RIGHT, ON_LEFT, ON_Y = range(6)
AT4, AT1, AT3, AT2K, AT2V, ATT = range(6)


def inverse_frequency():
    table = []
    for number in range(HEAD_SIZE // 2):
        base_freq = 500000.0 ** (-(2.0 * number) / HEAD_SIZE)
        wavelength = 2.0 * math.pi / base_freq
        smooth = (8192.0 / wavelength - 1.0) / 3.0
        if wavelength < 2048.0:
            table.append(base_freq)
        elif wavelength > 8192.0:
            table.append(base_freq / 8.0)
        else:
            table.append((1.0 - smooth) * base_freq / 8.0 + smooth * base_freq)
    return np.asarray(table, dtype=np.float32).astype(np.float64)


def rotary_tables():
    freq = np.concatenate([inverse_frequency()] * 2)
    rows = np.arange(TOK)[:, None] * freq
    starts = (np.arange(N_SEQ) * TOK)[:, None] * freq
    return np.concatenate(
        [np.cos(rows), np.sin(rows), np.cos(starts), np.sin(starts)]
    ).astype(np.float32)


def kernel(
    x_hbm, docs, wq_hbm, wk_hbm, wv_hbm, wo_hbm, tab_hbm,
    out,
    x, wkv, wq, wo, q, kv, acc, send, recv, att, bias, tab, rope,
    x_sem, wkv_sem, wq_sem, wo_sem, tab_sem,
    xs_sem, xr_sem, kv_send, kv_recv, red_send, red_recv,
):
    seq = lax.axis_index("seq")
    head = lax.axis_index("head")
    other = 1 - head
    place = lax.rem(seq, X_RING)
    right = jnp.where(place == X_RING - 1, seq - (X_RING - 1), seq + 1)
    left = jnp.where(place == 0, seq + (X_RING - 1), seq - 1)
    later = lax.rem(seq + X_RING, N_SEQ)
    earlier = lax.rem(seq + N_SEQ - X_RING, N_SEQ)
    own_rows = pl.ds(pl.multiple_of(head * HALF, HALF), HALF)
    other_rows = pl.ds(pl.multiple_of(other * HALF, HALF), HALF)

    x_copy = pltpu.make_async_copy(x_hbm, x.at[own_rows, :], x_sem)
    tab_copy = pltpu.make_async_copy(tab_hbm, tab, tab_sem)

    def lanes(number, size):
        return pl.ds(pl.multiple_of(number * size, size), size)

    def wkv_copies(h):
        return (
            pltpu.make_async_copy(
                wk_hbm.at[:, lanes(h, HEAD_SIZE)], wkv.at[h, :, pl.ds(0, HEAD_SIZE)], wkv_sem.at[h, 0]
            ),
            pltpu.make_async_copy(
                wv_hbm.at[:, lanes(h, HEAD_SIZE)],
                wkv.at[h, :, pl.ds(HEAD_SIZE, HEAD_SIZE)],
                wkv_sem.at[h, 1],
            ),
        )

    def wq_copy(h):
        return pltpu.make_async_copy(
            wq_hbm.at[:, lanes(h, GROUP * HEAD_SIZE)], wq.at[h], wq_sem.at[h]
        )

    def wo_copy(h):
        return pltpu.make_async_copy(
            wo_hbm.at[lanes(h, GROUP * HEAD_SIZE), :], wo.at[h], wo_sem.at[h]
        )

    x_copy.start()
    tab_copy.start()
    for h in range(KV_HERE):
        for copy in wkv_copies(h):
            copy.start()

    barrier = pltpu.get_barrier_semaphore()
    for target in ((seq, other), (right, head), (left, head), (later, head), (earlier, head)):
        pl.semaphore_signal(barrier, inc=1, device_id=target, device_id_type=MESH)
    pl.semaphore_wait(barrier, 5)

    def x_exchange():
        return pltpu.make_async_remote_copy(
            src_ref=x_hbm,
            dst_ref=x.at[own_rows, :],
            send_sem=xs_sem,
            recv_sem=xr_sem,
            device_id=(seq, other),
            device_id_type=MESH,
        )

    x_exchange().start()

    base = seq * TOK
    position = base + lax.broadcasted_iota(jnp.int32, (8, TOK), 1)

    def next_doc(number, state):
        end, start = state
        end = end + docs[number]
        return end, jnp.where(end <= position, end, start)

    _, start_row = lax.fori_loop(
        0, DOCS, next_doc, (jnp.int32(0), jnp.zeros((8, TOK), jnp.int32))
    )
    start_row = start_row.astype(jnp.float32)
    start = jnp.transpose(jnp.concatenate([start_row] * (HEAD_SIZE // 8), axis=0))
    base_f = base.astype(jnp.float32)
    lane = lax.broadcasted_iota(jnp.int32, (TOK, HEAD_SIZE), 1)
    row = lax.broadcasted_iota(jnp.int32, (TOK, HEAD_SIZE), 0)
    for slot in range(SLOTS):
        for half in range(TOK // HEAD_SIZE):
            offset = lane + half * HEAD_SIZE
            allowed = offset.astype(jnp.float32) + (base_f - float(slot * TOK)) >= start
            if slot == 0:
                allowed = allowed & (offset <= row)
            bias[:, pl.ds(slot * TOK + half * HEAD_SIZE, HEAD_SIZE)] = jnp.where(
                allowed, 0.0, NEG_FILL
            )

    tab_copy.wait()
    cos_row, sin_row = tab[pl.ds(0, TOK), :], tab[pl.ds(TOK, TOK), :]
    cos_base = tab[pl.ds(2 * TOK + seq, 1), :]
    sin_base = tab[pl.ds(2 * TOK + N_SEQ + seq, 1), :]
    cosine = cos_row * cos_base - sin_row * sin_base
    sine = sin_row * cos_base + cos_row * sin_base
    sine = jnp.where(lane < HEAD_SIZE // 2, -sine, sine)
    scale = HEAD_SIZE ** (-0.5) * math.log2(math.e)
    rope[0] = cosine
    rope[1] = sine
    rope[2] = cosine * scale
    rope[3] = sine * scale

    def rotated(value, which):
        turned = pltpu.roll(value, HEAD_SIZE // 2, 1)
        return (value * rope[which] + turned * rope[which + 1]).astype(jnp.bfloat16)

    def block(h, slot):
        return kv.at[:, h, lanes(slot, TOK), :]

    def part(which, h, slot):
        return kv.at[which, h, lanes(slot, TOK), :]

    def remote(source, target, h, sending, receiving, device):
        return pltpu.make_async_remote_copy(
            src_ref=source,
            dst_ref=target,
            send_sem=kv_send.at[h, sending],
            recv_sem=kv_recv.at[h, receiving],
            device_id=(device, head),
            device_id_type=MESH,
        )

    def to_later(h):
        return remote(block(h, 0), block(h, 4), h, TO_Y, AT4, later)

    def to_right(h, slot):
        return remote(block(h, slot), block(h, 1), h, TO_RIGHT, AT1, right)

    def to_left(h, slot):
        return remote(block(h, slot), block(h, 3), h, TO_LEFT, AT3, left)

    last = place == X_RING - 1
    first = place == 0

    def on_right(h):
        return remote(
            part(0, h, 1), part(0, h, jnp.where(last, 5, 2)), h, ON_RIGHT,
            jnp.where(last, ATT, AT2K), right,
        )

    def on_left(h):
        return remote(
            part(1, h, 3), part(1, h, jnp.where(first, 5, 2)), h, ON_LEFT,
            jnp.where(first, ATT, AT2V), left,
        )

    def key_on_later(h):
        return remote(part(0, h, 5), part(0, h, 2), h, ON_Y, AT2K, later)

    def value_on_earlier(h):
        return remote(part(1, h, 5), part(1, h, 2), h, ON_Y, AT2V, earlier)

    def stage_a(h):
        to_later(h).start()

        @pl.when(jnp.logical_not(last))
        def _():
            to_right(h, 0).start()

        @pl.when(first)
        def _():
            to_left(h, 0).start()

    def stage_b(h):
        to_later(h).wait_recv()

        @pl.when(last)
        def _():
            to_right(h, 4).start()

        @pl.when(jnp.logical_not(first))
        def _():
            to_left(h, 4).start()

    def stage_c(h):
        to_right(h, 0).wait_recv()
        on_right(h).start()
        to_left(h, 0).wait_recv()
        on_left(h).start()

    def stage_d(h):
        @pl.when(first)
        def _():
            remote(part(0, h, 5), part(0, h, 5), h, ON_Y, ATT, later).wait_recv()
            key_on_later(h).start()

        @pl.when(last)
        def _():
            remote(part(1, h, 5), part(1, h, 5), h, ON_Y, ATT, earlier).wait_recv()
            value_on_earlier(h).start()

    x_copy.wait()
    x_exchange().wait()

    def project_kv(h, carry):
        for copy in wkv_copies(h):
            copy.wait()
        wq_copy(h).start()
        both = jnp.dot(x[...], wkv[h], preferred_element_type=jnp.float32)
        kv[0, h, pl.ds(0, TOK), :] = rotated(both[:, :HEAD_SIZE], 0)
        kv[1, h, pl.ds(0, TOK), :] = both[:, HEAD_SIZE:].astype(jnp.bfloat16)
        stage_a(h)
        return carry

    lax.fori_loop(0, KV_HERE, project_kv, 0)

    def project_q(h, carry):
        wq_copy(h).wait()
        wo_copy(h).start()
        some = jnp.dot(x[...], wq[h], preferred_element_type=jnp.float32)
        for number in range(GROUP):
            q[h * GROUP + number] = rotated(
                some[:, number * HEAD_SIZE : (number + 1) * HEAD_SIZE], 2
            )
        stage_b(h)

        @pl.when(h >= 1)
        def _():
            stage_c(h - 1)

        @pl.when(h >= 2)
        def _():
            stage_d(h - 2)

        return carry

    lax.fori_loop(0, KV_HERE, project_q, 0)
    stage_c(KV_HERE - 1)
    stage_d(KV_HERE - 2)
    stage_d(KV_HERE - 1)

    def reduce_copy(chunk):
        return pltpu.make_async_remote_copy(
            src_ref=send.at[chunk],
            dst_ref=recv.at[chunk],
            send_sem=red_send.at[chunk],
            recv_sem=red_recv.at[chunk],
            device_id=(seq, other),
            device_id_type=MESH,
        )

    acc[...] = jnp.zeros_like(acc)

    def attend(h, carry):
        remote(part(0, h, 2), part(0, h, 2), h, ON_Y, AT2K, later).wait_recv()
        remote(part(1, h, 2), part(1, h, 2), h, ON_Y, AT2V, later).wait_recv()

        def one_head(number, inner):
            keys = kv[0, h, pl.ds(0, SLOTS * TOK), :]
            values = kv[1, h, pl.ds(0, SLOTS * TOK), :]
            values = jnp.concatenate([values, jnp.ones_like(values)], axis=1)
            score = lax.dot_general(
                q[h * GROUP + number], keys, (((1,), (1,)), ((), ())),
                preferred_element_type=jnp.float32,
            )
            score = score + bias[...]
            rowmax = jnp.max(score, axis=1, keepdims=True)
            weight = jnp.exp2(score - rowmax).astype(jnp.bfloat16)
            mixed = jnp.dot(weight, values, preferred_element_type=jnp.float32)
            att[:, lanes(number, HEAD_SIZE)] = (
                mixed[:, :HEAD_SIZE] / mixed[:, HEAD_SIZE:]
            ).astype(jnp.bfloat16)
            return inner

        lax.fori_loop(0, GROUP, one_head, 0)
        wo_copy(h).wait()

        def project_out(chunk, inner):
            columns = lanes(chunk, COLS)
            acc[:, columns] += jnp.dot(
                att[...], wo[h, :, columns], preferred_element_type=jnp.float32
            )

            @pl.when(h == KV_HERE - 1)
            def _():
                send[chunk] = acc[other_rows, columns].astype(jnp.bfloat16)
                reduce_copy(chunk).start()

            return inner

        lax.fori_loop(0, CHUNKS, project_out, 0)
        return carry

    lax.fori_loop(0, KV_HERE, attend, 0)

    def finish(chunk, carry):
        columns = lanes(chunk, COLS)
        reduce_copy(chunk).wait()
        out[:, columns] = (
            acc[own_rows, columns] + recv[chunk].astype(jnp.float32)
        ).astype(jnp.bfloat16)
        return carry

    lax.fori_loop(0, CHUNKS, finish, 0)

    def sent(h, carry):
        to_later(h).wait_send()
        to_right(h, 0).wait_send()
        to_left(h, 0).wait_send()
        on_right(h).wait_send()
        on_left(h).wait_send()

        @pl.when(first)
        def _():
            key_on_later(h).wait_send()

        @pl.when(last)
        def _():
            value_on_earlier(h).wait_send()

        return carry

    lax.fori_loop(0, KV_HERE, sent, 0)


def body(input_rows, doc_lengths, w_query, key_weight, value_weight, w_out):
    table = jnp.asarray(rotary_tables())
    hbm = pl.BlockSpec(memory_space=pl.ANY)
    dma = pltpu.SemaphoreType.DMA
    wide = GROUP * HEAD_SIZE
    return pl.pallas_call(
        kernel,
        out_shape=jax.ShapeDtypeStruct((HALF, WIDTH), jnp.bfloat16),
        in_specs=[hbm, pl.BlockSpec(memory_space=pltpu.SMEM), hbm, hbm, hbm, hbm, hbm],
        out_specs=pl.BlockSpec(memory_space=pltpu.VMEM),
        scratch_shapes=[
            pltpu.VMEM((TOK, WIDTH), jnp.bfloat16),
            pltpu.VMEM((KV_HERE, WIDTH, 2 * HEAD_SIZE), jnp.bfloat16),
            pltpu.VMEM((KV_HERE, WIDTH, wide), jnp.bfloat16),
            pltpu.VMEM((KV_HERE, wide, WIDTH), jnp.bfloat16),
            pltpu.VMEM((KV_HERE * GROUP, TOK, HEAD_SIZE), jnp.bfloat16),
            pltpu.VMEM((2, KV_HERE, (SLOTS + 1) * TOK, HEAD_SIZE), jnp.bfloat16),
            pltpu.VMEM((TOK, WIDTH), jnp.float32),
            pltpu.VMEM((CHUNKS, HALF, COLS), jnp.bfloat16),
            pltpu.VMEM((CHUNKS, HALF, COLS), jnp.bfloat16),
            pltpu.VMEM((TOK, wide), jnp.bfloat16),
            pltpu.VMEM((TOK, SLOTS * TOK), jnp.float32),
            pltpu.VMEM((2 * TOK + 2 * N_SEQ, HEAD_SIZE), jnp.float32),
            pltpu.VMEM((4, TOK, HEAD_SIZE), jnp.float32),
            dma(()), dma((KV_HERE, 2)), dma((KV_HERE,)), dma((KV_HERE,)), dma(()),
            dma(()), dma(()), dma((KV_HERE, 6)), dma((KV_HERE, 6)), dma((CHUNKS,)), dma((CHUNKS,)),
        ],
        compiler_params=pltpu.CompilerParams(
            collective_id=0, has_side_effects=True, vmem_limit_bytes=62 << 20
        ),
        name="layer",
    )(input_rows, doc_lengths, w_query, key_weight, value_weight, w_out, table)


def solution(mesh):
    in_specs = (
        P(("seq", "head"), None),
        P(),
        P(None, "head"),
        P(None, "head"),
        P(None, "head"),
        P("head", None),
    )
    out_specs = P(("seq", "head"), None)
    return jax.shard_map(body, mesh=mesh, in_specs=in_specs, out_specs=out_specs, check_vma=False)
```

time: 154 us -> 70.5 us (0.46)
  the two profiles are of different devices: /device:TPU:1 before, /device:TPU:7 now
where the time goes in v1:
time: 70.5 us; the launch traced here: 70.4 us
  Pallas kernels  68.1 us (97%)
  local copies, waits for them, and re-layouts  2.29 us (3%)
    pallas_call x1, Pallas kernels, body(): pl.pallas_call(kernel, out_shape=jax.ShapeDtypeStruct((HALF, WIDTH), jnp....  68.1 us
    unnamed x1, local copies, waits for them, and re-layouts  2.29 us

profile of v1, /device:TPU:7, one launch (start us, length us, event | category | flops | bytes accessed | tf_op | source)
XLA Modules:
  0.0 70.4 jit_solution(8469733018611137875)
XLA Ops:
  0.0 68.1 %layer.1 = bf16[128,4096]{1,0:T(8,128)(2,1)} custom-call(bf16[128,4096]{1,0:T(8,128)(2,1)} %x_hbm.1, s32[64]{0:T(128)} %docs.1, bf16[4096,2048]{1,0:T(8,128)(2,1)} %wq_hbm.1, bf16[4096,512]{1,0:T(8,128)(2,1)} %wk_hbm.1, bf16[4096,512]{1,0:T(8,128)(2,1)} %wv_hbm.1, bf16[2048,4096]{1,0:T(8,128)(2,1)} %wo_hbm.1, f32[768,128]{1,0:T(8,128)} %constant.2.clone.tab_hbm), custom_call_target="tpu_custom_call" | custom-call | tf_op jit(solution)/shard_map/layer/pallas_call | solution.py:380
  68.1 2.3 %copy.9 = bf16[128,4096]{1,0:T(8,128)(2,1)} copy(bf16[128,4096]{1,0:T(8,128)(2,1)} %layer.1) | data formatting | bytes 2097152

commit v2 on v1

--- a/solution.py
+++ b/solution.py
@@ -20,8 +20,9 @@
 N_SEQ = 128
 DOCS = 64
 NEG_FILL = -1e30
-COLS = 512
+COLS = 1024
 CHUNKS = WIDTH // COLS
+WIDE_COLS = 2048
 
 TO_Y, TO_RIGHT, TO_LEFT, ON_RIGHT, ON_LEFT, ON_Y = range(6)
 AT4, AT1, AT3, AT2K, AT2V, ATT = range(6)
@@ -64,8 +65,12 @@
     place = lax.rem(seq, X_RING)
     right = jnp.where(place == X_RING - 1, seq - (X_RING - 1), seq + 1)
     left = jnp.where(place == 0, seq + (X_RING - 1), seq - 1)
-    later = lax.rem(seq + X_RING, N_SEQ)
-    earlier = lax.rem(seq + N_SEQ - X_RING, N_SEQ)
+    has_later = seq < N_SEQ - X_RING
+    has_earlier = seq >= X_RING
+    later = jnp.where(has_later, seq + X_RING, seq)
+    earlier = jnp.where(has_earlier, seq - X_RING, seq)
+    gives_far = seq == N_SEQ - 3
+    takes_far = seq == N_SEQ - 1
     own_rows = pl.ds(pl.multiple_of(head * HALF, HALF), HALF)
     other_rows = pl.ds(pl.multiple_of(other * HALF, HALF), HALF)
 
@@ -104,9 +109,32 @@
             copy.start()
 
     barrier = pltpu.get_barrier_semaphore()
-    for target in ((seq, other), (right, head), (left, head), (later, head), (earlier, head)):
+
+    def greet(target):
         pl.semaphore_signal(barrier, inc=1, device_id=target, device_id_type=MESH)
-    pl.semaphore_wait(barrier, 5)
+
+    for target in ((seq, other), (right, head), (left, head)):
+        greet(target)
+
+    @pl.when(has_later)
+    def _():
+        greet((later, head))
+
+    @pl.when(has_earlier)
+    def _():
+        greet((earlier, head))
+
+    @pl.when(gives_far)
+    def _():
+        greet((seq + 2, head))
+
+    @pl.when(takes_far)
+    def _():
+        greet((seq - 2, head))
+
+    callers = 3 + has_later.astype(jnp.int32) + has_earlier.astype(jnp.int32)
+    callers = callers + gives_far.astype(jnp.int32) + takes_far.astype(jnp.int32)
+    pl.semaphore_wait(barrier, callers)
 
     def x_exchange():
         return pltpu.make_async_remote_copy(
@@ -209,8 +237,17 @@
     def value_on_earlier(h):
         return remote(part(1, h, 5), part(1, h, 2), h, ON_Y, AT2V, earlier)
 
+    def value_far(h):
+        return remote(part(1, h, 0), part(1, h, 2), h, ON_Y, AT2V, seq + 2)
+
     def stage_a(h):
-        to_later(h).start()
+        @pl.when(has_later)
+        def _():
+            to_later(h).start()
+
+        @pl.when(gives_far)
+        def _():
+            value_far(h).start()
 
         @pl.when(jnp.logical_not(last))
         def _():
@@ -221,7 +258,9 @@
             to_left(h, 0).start()
 
     def stage_b(h):
-        to_later(h).wait_recv()
+        @pl.when(has_earlier)
+        def _():
+            to_later(h).wait_recv()
 
         @pl.when(last)
         def _():
@@ -241,12 +280,26 @@
         @pl.when(first)
         def _():
             remote(part(0, h, 5), part(0, h, 5), h, ON_Y, ATT, later).wait_recv()
-            key_on_later(h).start()
+
+            @pl.when(has_later)
+            def _():
+                key_on_later(h).start()
 
         @pl.when(last)
         def _():
             remote(part(1, h, 5), part(1, h, 5), h, ON_Y, ATT, earlier).wait_recv()
-            value_on_earlier(h).start()
+
+            @pl.when(has_earlier)
+            def _():
+                value_on_earlier(h).start()
+
+    @pl.when(jnp.logical_not(has_earlier))
+    def _():
+        kv[:, :, pl.ds(4 * TOK, TOK), :] = jnp.zeros((2, KV_HERE, TOK, HEAD_SIZE), jnp.bfloat16)
+
+    @pl.when(seq == 0)
+    def _():
+        kv[0, :, pl.ds(2 * TOK, TOK), :] = jnp.zeros((KV_HERE, TOK, HEAD_SIZE), jnp.bfloat16)
 
     x_copy.wait()
     x_exchange().wait()
@@ -301,13 +354,15 @@
     acc[...] = jnp.zeros_like(acc)
 
     def attend(h, carry):
-        remote(part(0, h, 2), part(0, h, 2), h, ON_Y, AT2K, later).wait_recv()
+        @pl.when(seq > 0)
+        def _():
+            remote(part(0, h, 2), part(0, h, 2), h, ON_Y, AT2K, later).wait_recv()
+
         remote(part(1, h, 2), part(1, h, 2), h, ON_Y, AT2V, later).wait_recv()
-
-        def one_head(number, inner):
-            keys = kv[0, h, pl.ds(0, SLOTS * TOK), :]
-            values = kv[1, h, pl.ds(0, SLOTS * TOK), :]
-            values = jnp.concatenate([values, jnp.ones_like(values)], axis=1)
+        keys = kv[0, h, pl.ds(0, SLOTS * TOK), :]
+        values = kv[1, h, pl.ds(0, SLOTS * TOK), :]
+        values = jnp.concatenate([values, jnp.ones_like(values)], axis=1)
+        for number in range(GROUP):
             score = lax.dot_general(
                 q[h * GROUP + number], keys, (((1,), (1,)), ((), ())),
                 preferred_element_type=jnp.float32,
@@ -316,31 +371,36 @@
             rowmax = jnp.max(score, axis=1, keepdims=True)
             weight = jnp.exp2(score - rowmax).astype(jnp.bfloat16)
             mixed = jnp.dot(weight, values, preferred_element_type=jnp.float32)
-            att[:, lanes(number, HEAD_SIZE)] = (
+            att[:, number * HEAD_SIZE : (number + 1) * HEAD_SIZE] = (
                 mixed[:, :HEAD_SIZE] / mixed[:, HEAD_SIZE:]
             ).astype(jnp.bfloat16)
-            return inner
-
-        lax.fori_loop(0, GROUP, one_head, 0)
         wo_copy(h).wait()
 
         def project_out(chunk, inner):
-            columns = lanes(chunk, COLS)
+            columns = lanes(chunk, WIDE_COLS)
             acc[:, columns] += jnp.dot(
                 att[...], wo[h, :, columns], preferred_element_type=jnp.float32
             )
-
-            @pl.when(h == KV_HERE - 1)
-            def _():
-                send[chunk] = acc[other_rows, columns].astype(jnp.bfloat16)
-                reduce_copy(chunk).start()
-
             return inner
 
-        lax.fori_loop(0, CHUNKS, project_out, 0)
+        @pl.when(h < KV_HERE - 1)
+        def _():
+            lax.fori_loop(0, WIDTH // WIDE_COLS, project_out, 0)
+
         return carry
 
     lax.fori_loop(0, KV_HERE, attend, 0)
+
+    def project_last(chunk, carry):
+        columns = lanes(chunk, COLS)
+        acc[:, columns] += jnp.dot(
+            att[...], wo[KV_HERE - 1, :, columns], preferred_element_type=jnp.float32
+        )
+        send[chunk] = acc[other_rows, columns].astype(jnp.bfloat16)
+        reduce_copy(chunk).start()
+        return carry
+
+    lax.fori_loop(0, CHUNKS, project_last, 0)
 
     def finish(chunk, carry):
         columns = lanes(chunk, COLS)
@@ -353,17 +413,24 @@
     lax.fori_loop(0, CHUNKS, finish, 0)
 
     def sent(h, carry):
-        to_later(h).wait_send()
+        @pl.when(has_later)
+        def _():
+            to_later(h).wait_send()
+
+        @pl.when(gives_far)
+        def _():
+            value_far(h).wait_send()
+
         to_right(h, 0).wait_send()
         to_left(h, 0).wait_send()
         on_right(h).wait_send()
         on_left(h).wait_send()
 
-        @pl.when(first)
+        @pl.when(first & has_later)
         def _():
             key_on_later(h).wait_send()
 
-        @pl.when(last)
+        @pl.when(last & has_earlier)
         def _():
             value_on_earlier(h).wait_send()
 

time: 70.5 us -> 59.6 us (0.85)
  the two profiles are of different devices: /device:TPU:7 before, /device:TPU:255 now
where the time goes in v2:
time: 59.6 us; the launch traced here: 59.4 us
  Pallas kernels  57.1 us (96%)
  local copies, waits for them, and re-layouts  2.29 us (4%)
    pallas_call x1, Pallas kernels, body(): pl.pallas_call(kernel, out_shape=jax.ShapeDtypeStruct((HALF, WIDTH), jnp....  57.1 us
    unnamed x1, local copies, waits for them, and re-layouts  2.29 us

profile of v2, /device:TPU:255, one launch (start us, length us, event | category | flops | bytes accessed | tf_op | source)
XLA Modules:
  0.0 59.4 jit_solution(16015148521798572359)
XLA Ops:
  0.0 57.1 %layer.1 = bf16[128,4096]{1,0:T(8,128)(2,1)} custom-call(bf16[128,4096]{1,0:T(8,128)(2,1)} %x_hbm.1, s32[64]{0:T(128)} %docs.1, bf16[4096,2048]{1,0:T(8,128)(2,1)} %wq_hbm.1, bf16[4096,512]{1,0:T(8,128)(2,1)} %wk_hbm.1, bf16[4096,512]{1,0:T(8,128)(2,1)} %wv_hbm.1, bf16[2048,4096]{1,0:T(8,128)(2,1)} %wo_hbm.1, f32[768,128]{1,0:T(8,128)} %constant.2.clone.tab_hbm), custom_call_target="tpu_custom_call" | custom-call | tf_op jit(solution)/shard_map/layer/pallas_call | solution.py:447
  57.2 2.3 %copy.9 = bf16[128,4096]{1,0:T(8,128)(2,1)} copy(bf16[128,4096]{1,0:T(8,128)(2,1)} %layer.1) | data formatting | bytes 2097152

commit v3 on v2

v3 whole, which is shorter than its diff:
```python
import math

import jax
import jax.numpy as jnp
import numpy as np
from jax import lax
from jax.experimental import pallas as pl
from jax.experimental.pallas import tpu as pltpu
from jax.sharding import PartitionSpec as P

MESH = pl.DeviceIdType.MESH
HEAD_SIZE = 128
TOK = 256
HALF = 128
WIDTH = 4096
KV_HERE = 4
GROUP = 4
SLOTS = 5
X_RING = 4
N_SEQ = 128
DOCS = 64
NEG_FILL = -1e30
COLS = 1024
CHUNKS = WIDTH // COLS
WIDE_COLS = 2048

AT1, AT2, AT3, AT4 = 1, 2, 3, 4
UNITS = 2 * KV_HERE


def inverse_frequency():
    table = []
    for number in range(HEAD_SIZE // 2):
        base_freq = 500000.0 ** (-(2.0 * number) / HEAD_SIZE)
        wavelength = 2.0 * math.pi / base_freq
        smooth = (8192.0 / wavelength - 1.0) / 3.0
        if wavelength < 2048.0:
            table.append(base_freq)
        elif wavelength > 8192.0:
            table.append(base_freq / 8.0)
        else:
            table.append((1.0 - smooth) * base_freq / 8.0 + smooth * base_freq)
    return np.asarray(table, dtype=np.float32).astype(np.float64)


def rotary_tables():
    freq = np.concatenate([inverse_frequency()] * 2)
    rows = np.arange(TOK)[:, None] * freq
    starts = (np.arange(N_SEQ) * TOK)[:, None] * freq
    return np.concatenate(
        [np.cos(rows), np.sin(rows), np.cos(starts), np.sin(starts)]
    ).astype(np.float32)


def kernel(
    x_hbm, docs, wq_hbm, wk_hbm, wv_hbm, wo_hbm, tab_hbm,
    out,
    x, wkv, wq, wo, q, kv, acc, send, recv, att, bias, tab, rope,
    x_sem, wkv_sem, wq_sem, wo_sem, tab_sem,
    xs_sem, xr_sem, kv_send, kv_recv, red_send, red_recv,
):
    seq = lax.axis_index("seq")
    head = lax.axis_index("head")
    other = 1 - head
    place = lax.rem(seq, X_RING)
    right = jnp.where(place == X_RING - 1, seq - (X_RING - 1), seq + 1)
    left = jnp.where(place == 0, seq + (X_RING - 1), seq - 1)
    first = place == 0
    last = place == X_RING - 1
    low = place < X_RING // 2
    far = jnp.where(low, seq + 2, seq - 2)
    has_later = seq < N_SEQ - X_RING
    has_earlier = seq >= X_RING
    later = jnp.where(has_later, seq + X_RING, seq)
    earlier = jnp.where(has_earlier, seq - X_RING, seq)
    own_rows = pl.ds(pl.multiple_of(head * HALF, HALF), HALF)
    other_rows = pl.ds(pl.multiple_of(other * HALF, HALF), HALF)

    x_copy = pltpu.make_async_copy(x_hbm, x.at[own_rows, :], x_sem)
    tab_copy = pltpu.make_async_copy(tab_hbm, tab, tab_sem)

    def lanes(number, size):
        return pl.ds(pl.multiple_of(number * size, size), size)

    def wkv_copies(h):
        return (
            pltpu.make_async_copy(
                wk_hbm.at[:, lanes(h, HEAD_SIZE)], wkv.at[h, :, pl.ds(0, HEAD_SIZE)], wkv_sem.at[h, 0]
            ),
            pltpu.make_async_copy(
                wv_hbm.at[:, lanes(h, HEAD_SIZE)],
                wkv.at[h, :, pl.ds(HEAD_SIZE, HEAD_SIZE)],
                wkv_sem.at[h, 1],
            ),
        )

    def wq_copy(h):
        return pltpu.make_async_copy(
            wq_hbm.at[:, lanes(h, GROUP * HEAD_SIZE)], wq.at[h], wq_sem.at[h]
        )

    def wo_copy(h):
        return pltpu.make_async_copy(
            wo_hbm.at[lanes(h, GROUP * HEAD_SIZE), :], wo.at[h], wo_sem.at[h]
        )

    x_copy.start()
    tab_copy.start()
    for h in range(KV_HERE):
        for copy in wkv_copies(h):
            copy.start()

    barrier = pltpu.get_barrier_semaphore()

    def greet(target):
        pl.semaphore_signal(barrier, inc=1, device_id=target, device_id_type=MESH)

    for target in ((seq, other), (right, head), (left, head), (far, head)):
        greet(target)

    @pl.when(has_later)
    def _():
        greet((later, head))

    @pl.when(has_earlier)
    def _():
        greet((earlier, head))

    def x_exchange():
        return pltpu.make_async_remote_copy(
            src_ref=x_hbm,
            dst_ref=x.at[own_rows, :],
            send_sem=xs_sem,
            recv_sem=xr_sem,
            device_id=(seq, other),
            device_id_type=MESH,
        )

    lane = lax.broadcasted_iota(jnp.int32, (TOK, HEAD_SIZE), 1)
    row = lax.broadcasted_iota(jnp.int32, (TOK, HEAD_SIZE), 0)

    tab_copy.wait()
    cos_row, sin_row = tab[pl.ds(0, TOK), :], tab[pl.ds(TOK, TOK), :]
    cos_base = tab[pl.ds(2 * TOK + seq, 1), :]
    sin_base = tab[pl.ds(2 * TOK + N_SEQ + seq, 1), :]
    cosine = cos_row * cos_base - sin_row * sin_base
    sine = sin_row * cos_base + cos_row * sin_base
    sine = jnp.where(lane < HEAD_SIZE // 2, -sine, sine)
    scale = HEAD_SIZE ** (-0.5) * math.log2(math.e)
    rope[0] = cosine
    rope[1] = sine
    rope[2] = cosine * scale
    rope[3] = sine * scale

    def rotated(value, which, rows):
        turned = pltpu.roll(value, HEAD_SIZE // 2, 1)
        return (value * rope[which, rows] + turned * rope[which + 1, rows]).astype(jnp.bfloat16)

    def unit_rows(half, slot):
        core = head if half == 0 else other
        return pl.ds(pl.multiple_of(slot * TOK + core * HALF, HALF), HALF)

    def remote(half, h, source, target, device):
        return pltpu.make_async_remote_copy(
            src_ref=kv.at[:, h, unit_rows(half, source), :],
            dst_ref=kv.at[:, h, unit_rows(half, target), :],
            send_sem=kv_send.at[half * KV_HERE + h, target],
            recv_sem=kv_recv.at[half * KV_HERE + h, target],
            device_id=(device, head),
            device_id_type=MESH,
        )

    def send_own(half, h):
        @pl.when(has_later)
        def _():
            remote(half, h, 0, AT4, later).start()

        @pl.when(jnp.logical_not(last))
        def _():
            remote(half, h, 0, AT1, right).start()

        @pl.when(first)
        def _():
            remote(half, h, 0, AT3, left).start()

        @pl.when(low)
        def _():
            remote(half, h, 0, AT2, far).start()

    def pass_on(half, h):
        @pl.when(has_earlier)
        def _():
            remote(half, h, 0, AT4, later).wait_recv()

        @pl.when(jnp.logical_not(first))
        def _():
            remote(half, h, 4, AT3, left).start()

        @pl.when(last)
        def _():
            remote(half, h, 4, AT1, right).start()

        @pl.when(jnp.logical_not(low))
        def _():
            remote(half, h, 4, AT2, far).start()

    def project_kv(half, h):
        rows = own_rows if half == 0 else other_rows
        both = jnp.dot(x[rows, :], wkv[h], preferred_element_type=jnp.float32)
        kv[0, h, unit_rows(half, 0), :] = rotated(both[:, :HEAD_SIZE], 0, rows)
        kv[1, h, unit_rows(half, 0), :] = both[:, HEAD_SIZE:].astype(jnp.bfloat16)

    def project_own(h, carry):
        for copy in wkv_copies(h):
            copy.wait()
        wq_copy(h).start()
        project_kv(0, h)
        return carry

    x_copy.wait()
    lax.fori_loop(0, 2, project_own, 0)

    callers = 4 + has_later.astype(jnp.int32) + has_earlier.astype(jnp.int32)
    pl.semaphore_wait(barrier, callers)
    x_exchange().start()
    send_own(0, 0)
    send_own(0, 1)
    lax.fori_loop(2, KV_HERE, project_own, 0)

    base = seq * TOK
    position = base + lax.broadcasted_iota(jnp.int32, (8, TOK), 1)

    def next_doc(number, state):
        end, start = state
        end = end + docs[number]
        return end, jnp.where(end <= position, end, start)

    _, start_row = lax.fori_loop(
        0, DOCS, next_doc, (jnp.int32(0), jnp.zeros((8, TOK), jnp.int32))
    )
    start_row = start_row.astype(jnp.float32)
    start = jnp.transpose(jnp.concatenate([start_row] * (HEAD_SIZE // 8), axis=0))
    base_f = base.astype(jnp.float32)
    for slot in range(SLOTS):
        for half in range(TOK // HEAD_SIZE):
            offset = lane + half * HEAD_SIZE
            allowed = offset.astype(jnp.float32) + (base_f - float(slot * TOK)) >= start
            if slot == 0:
                allowed = allowed & (offset <= row)
            bias[:, pl.ds(slot * TOK + half * HEAD_SIZE, HEAD_SIZE)] = jnp.where(
                allowed, 0.0, NEG_FILL
            )

    @pl.when(jnp.logical_not(has_earlier))
    def _():
        kv[:, :, pl.ds(4 * TOK, TOK), :] = jnp.zeros((2, KV_HERE, TOK, HEAD_SIZE), jnp.bfloat16)

    acc[...] = jnp.zeros_like(acc)
    x_exchange().wait()

    def project_other(h, carry):
        @pl.when(h >= 2)
        def _():
            send_own(0, h)

        project_kv(1, h)
        send_own(1, h)
        return carry

    lax.fori_loop(0, KV_HERE, project_other, 0)
    pass_on(0, 0)

    def project_q(h, carry):
        wq_copy(h).wait()
        wo_copy(h).start()
        some = jnp.dot(x[...], wq[h], preferred_element_type=jnp.float32)
        for number in range(GROUP):
            q[h * GROUP + number] = rotated(
                some[:, number * HEAD_SIZE : (number + 1) * HEAD_SIZE], 2, slice(None)
            )
        for step, (half, head_number) in enumerate(((0, 1), (1, 0), (1, 1), (0, 2))):
            @pl.when(h == step)
            def _():
                pass_on(half, head_number)

        return carry

    lax.fori_loop(0, KV_HERE, project_q, 0)
    pass_on(1, 2)

    def reduce_copy(chunk):
        return pltpu.make_async_remote_copy(
            src_ref=send.at[chunk],
            dst_ref=recv.at[chunk],
            send_sem=red_send.at[chunk],
            recv_sem=red_recv.at[chunk],
            device_id=(seq, other),
            device_id_type=MESH,
        )

    def attend(h, carry):
        for half in range(2):
            for slot in (AT1, AT2, AT3):
                remote(half, h, 0, slot, far).wait_recv()
        keys = kv[0, h, pl.ds(0, SLOTS * TOK), :]
        values = kv[1, h, pl.ds(0, SLOTS * TOK), :]
        values = jnp.concatenate([values, jnp.ones_like(values)], axis=1)
        for number in range(GROUP):
            score = lax.dot_general(
                q[h * GROUP + number], keys, (((1,), (1,)), ((), ())),
                preferred_element_type=jnp.float32,
            )
            score = score + bias[...]
            rowmax = jnp.max(score, axis=1, keepdims=True)
            weight = jnp.exp2(score - rowmax).astype(jnp.bfloat16)
            mixed = jnp.dot(weight, values, preferred_element_type=jnp.float32)
            att[:, number * HEAD_SIZE : (number + 1) * HEAD_SIZE] = (
                mixed[:, :HEAD_SIZE] / mixed[:, HEAD_SIZE:]
            ).astype(jnp.bfloat16)

        @pl.when(h == 0)
        def _():
            pass_on(0, 3)
            pass_on(1, 3)

        wo_copy(h).wait()

        def project_out(chunk, inner):
            columns = lanes(chunk, WIDE_COLS)
            acc[:, columns] += jnp.dot(
                att[...], wo[h, :, columns], preferred_element_type=jnp.float32
            )
            return inner

        @pl.when(h < KV_HERE - 1)
        def _():
            lax.fori_loop(0, WIDTH // WIDE_COLS, project_out, 0)

        return carry

    lax.fori_loop(0, KV_HERE, attend, 0)

    def project_last(chunk, carry):
        columns = lanes(chunk, COLS)
        acc[:, columns] += jnp.dot(
            att[...], wo[KV_HERE - 1, :, columns], preferred_element_type=jnp.float32
        )
        send[chunk] = acc[other_rows, columns].astype(jnp.bfloat16)
        reduce_copy(chunk).start()
        return carry

    lax.fori_loop(0, CHUNKS, project_last, 0)

    def finish(chunk, carry):
        columns = lanes(chunk, COLS)
        reduce_copy(chunk).wait()
        out[:, columns] = (
            acc[own_rows, columns] + recv[chunk].astype(jnp.float32)
        ).astype(jnp.bfloat16)
        return carry

    lax.fori_loop(0, CHUNKS, finish, 0)

    def sent(h, carry):
        for half in range(2):
            @pl.when(has_later)
            def _():
                remote(half, h, 0, AT4, later).wait_send()

            for slot in (AT1, AT2, AT3):
                remote(half, h, 0, slot, far).wait_send()

        return carry

    lax.fori_loop(0, KV_HERE, sent, 0)


def body(input_rows, doc_lengths, w_query, key_weight, value_weight, w_out):
    table = jnp.asarray(rotary_tables())
    hbm = pl.BlockSpec(memory_space=pl.ANY)
    dma = pltpu.SemaphoreType.DMA
    wide = GROUP * HEAD_SIZE
    return pl.pallas_call(
        kernel,
        out_shape=jax.ShapeDtypeStruct((HALF, WIDTH), jnp.bfloat16),
        in_specs=[hbm, pl.BlockSpec(memory_space=pltpu.SMEM), hbm, hbm, hbm, hbm, hbm],
        out_specs=pl.BlockSpec(memory_space=pltpu.VMEM),
        scratch_shapes=[
            pltpu.VMEM((TOK, WIDTH), jnp.bfloat16),
            pltpu.VMEM((KV_HERE, WIDTH, 2 * HEAD_SIZE), jnp.bfloat16),
            pltpu.VMEM((KV_HERE, WIDTH, wide), jnp.bfloat16),
            pltpu.VMEM((KV_HERE, wide, WIDTH), jnp.bfloat16),
            pltpu.VMEM((KV_HERE * GROUP, TOK, HEAD_SIZE), jnp.bfloat16),
            pltpu.VMEM((2, KV_HERE, SLOTS * TOK, HEAD_SIZE), jnp.bfloat16),
            pltpu.VMEM((TOK, WIDTH), jnp.float32),
            pltpu.VMEM((CHUNKS, HALF, COLS), jnp.bfloat16),
            pltpu.VMEM((CHUNKS, HALF, COLS), jnp.bfloat16),
            pltpu.VMEM((TOK, wide), jnp.bfloat16),
            pltpu.VMEM((TOK, SLOTS * TOK), jnp.float32),
            pltpu.VMEM((2 * TOK + 2 * N_SEQ, HEAD_SIZE), jnp.float32),
            pltpu.VMEM((4, TOK, HEAD_SIZE), jnp.float32),
            dma(()), dma((KV_HERE, 2)), dma((KV_HERE,)), dma((KV_HERE,)), dma(()),
            dma(()), dma(()), dma((UNITS, SLOTS)), dma((UNITS, SLOTS)), dma((CHUNKS,)), dma((CHUNKS,)),
        ],
        compiler_params=pltpu.CompilerParams(
            collective_id=0, has_side_effects=True, vmem_limit_bytes=62 << 20
        ),
        name="layer",
    )(input_rows, doc_lengths, w_query, key_weight, value_weight, w_out, table)


def solution(mesh):
    in_specs = (
        P(("seq", "head"), None),
        P(),
        P(None, "head"),
        P(None, "head"),
        P(None, "head"),
        P("head", None),
    )
    out_specs = P(("seq", "head"), None)
    return jax.shard_map(body, mesh=mesh, in_specs=in_specs, out_specs=out_specs, check_vma=False)
```

time: 59.6 us -> 50.6 us (0.85)
  the two profiles are of different devices: /device:TPU:255 before, /device:TPU:225 now
where the time goes in v3:
time: 50.6 us; the launch traced here: 50.5 us
  Pallas kernels  48.2 us (95%)
  local copies, waits for them, and re-layouts  2.29 us (5%)
    pallas_call x1, Pallas kernels, body(): pl.pallas_call(kernel, out_shape=jax.ShapeDtypeStruct((HALF, WIDTH), jnp....  48.2 us
    unnamed x1, local copies, waits for them, and re-layouts  2.29 us

profile of v3, /device:TPU:225, one launch (start us, length us, event | category | flops | bytes accessed | tf_op | source)
XLA Modules:
  0.0 50.5 jit_solution(13278864150792441790)
XLA Ops:
  0.0 48.2 %layer.1 = bf16[128,4096]{1,0:T(8,128)(2,1)} custom-call(bf16[128,4096]{1,0:T(8,128)(2,1)} %x_hbm.1, s32[64]{0:T(128)} %docs.1, bf16[4096,2048]{1,0:T(8,128)(2,1)} %wq_hbm.1, bf16[4096,512]{1,0:T(8,128)(2,1)} %wk_hbm.1, bf16[4096,512]{1,0:T(8,128)(2,1)} %wv_hbm.1, bf16[2048,4096]{1,0:T(8,128)(2,1)} %wo_hbm.1, f32[768,128]{1,0:T(8,128)} %constant.2.clone.tab_hbm), custom_call_target="tpu_custom_call" | custom-call | tf_op jit(solution)/shard_map/layer/pallas_call | solution.py:383
  48.2 2.3 %copy.9 = bf16[128,4096]{1,0:T(8,128)(2,1)} copy(bf16[128,4096]{1,0:T(8,128)(2,1)} %layer.1) | data formatting | bytes 2097152

commit v4 on v3

--- a/solution.py
+++ b/solution.py
@@ -22,10 +22,17 @@
 NEG_FILL = -1e30
 COLS = 1024
 CHUNKS = WIDTH // COLS
+TILE = GROUP * HEAD_SIZE
+PLACES = 6
 WIDE_COLS = 2048
 
-AT1, AT2, AT3, AT4 = 1, 2, 3, 4
 UNITS = 2 * KV_HERE
+ORDER = ((0, 0), (0, 1), (1, 0), (1, 1), (0, 2), (1, 2), (0, 3), (1, 3))
+KEY, VALUE, BOTH = 0, 1, slice(None)
+PLACE_OF = (0, 1, 4, 2, 3)
+EARLY = 4 * TOK
+AT4, AT1, AT3, AT2K, AT2V = range(5)
+TO4, TO1, TO3, STRAIGHT, ON_RIGHT, ON_LEFT = range(6)
 
 
 def inverse_frequency():
@@ -55,7 +62,7 @@
 def kernel(
     x_hbm, docs, wq_hbm, wk_hbm, wv_hbm, wo_hbm, tab_hbm,
     out,
-    x, wkv, wq, wo, q, kv, acc, send, recv, att, bias, tab, rope,
+    x, wkv, weights, q, kv, acc, send, recv, att, bias, tab, rope, partial, top,
     x_sem, wkv_sem, wq_sem, wo_sem, tab_sem,
     xs_sem, xr_sem, kv_send, kv_recv, red_send, red_recv,
 ):
@@ -96,13 +103,35 @@
 
     def wq_copy(h):
         return pltpu.make_async_copy(
-            wq_hbm.at[:, lanes(h, GROUP * HEAD_SIZE)], wq.at[h], wq_sem.at[h]
+            wq_hbm.at[:, :, lanes(h, TILE)], weights.at[h], wq_sem.at[h]
         )
 
-    def wo_copy(h):
-        return pltpu.make_async_copy(
-            wo_hbm.at[lanes(h, GROUP * HEAD_SIZE), :], wo.at[h], wo_sem.at[h]
-        )
+    def wo_place(h):
+        return lax.rem(h + KV_HERE, PLACES)
+
+    def wo_copies(h):
+        return [
+            pltpu.make_async_copy(
+                wo_hbm.at[lanes(h, TILE), pl.ds(block * TILE, TILE)],
+                weights.at[wo_place(h), block], wo_sem.at[h, block],
+            )
+            for block in range(WIDTH // TILE)
+        ]
+
+    def start_all(copies):
+        for copy in copies:
+            copy.start()
+
+    def wait_all(copies):
+        for copy in copies:
+            copy.wait()
+
+    def projected_out(h, first_block, blocks):
+        place = wo_place(h)
+        return [
+            jnp.dot(att[...], weights[place, first_block + block], preferred_element_type=jnp.float32)
+            for block in range(blocks)
+        ]
 
     x_copy.start()
     tab_copy.start()
@@ -158,51 +187,88 @@
 
     def unit_rows(half, slot):
         core = head if half == 0 else other
-        return pl.ds(pl.multiple_of(slot * TOK + core * HALF, HALF), HALF)
-
-    def remote(half, h, source, target, device):
+        return pl.ds(pl.multiple_of(PLACE_OF[slot] * TOK + core * HALF, HALF), HALF)
+
+    def remote(unit, parts, source, target, leaving, landing, device):
+        half, h = unit
         return pltpu.make_async_remote_copy(
-            src_ref=kv.at[:, h, unit_rows(half, source), :],
-            dst_ref=kv.at[:, h, unit_rows(half, target), :],
-            send_sem=kv_send.at[half * KV_HERE + h, target],
-            recv_sem=kv_recv.at[half * KV_HERE + h, target],
+            src_ref=kv.at[parts, h, unit_rows(half, source), :],
+            dst_ref=kv.at[parts, h, unit_rows(half, target), :],
+            send_sem=kv_send.at[half * KV_HERE + h, leaving],
+            recv_sem=kv_recv.at[half * KV_HERE + h, landing],
             device_id=(device, head),
             device_id_type=MESH,
         )
 
+    def landed(unit, landing):
+        parts = (BOTH, BOTH, BOTH, KEY, VALUE)[landing]
+        slot = (4, 1, 3, 2, 2)[landing]
+        remote(unit, parts, slot, slot, TO4, landing, right).wait_recv()
+
     def send_own(half, h):
+        unit = (half, h)
+
         @pl.when(has_later)
         def _():
-            remote(half, h, 0, AT4, later).start()
+            remote(unit, BOTH, 0, 4, TO4, AT4, later).start()
 
         @pl.when(jnp.logical_not(last))
         def _():
-            remote(half, h, 0, AT1, right).start()
+            remote(unit, BOTH, 0, 1, TO1, AT1, right).start()
 
         @pl.when(first)
         def _():
-            remote(half, h, 0, AT3, left).start()
-
-        @pl.when(low)
-        def _():
-            remote(half, h, 0, AT2, far).start()
-
-    def pass_on(half, h):
+            remote(unit, BOTH, 0, 3, TO3, AT3, left).start()
+
+        @pl.when(place == 1)
+        def _():
+            remote(unit, KEY, 0, 2, STRAIGHT, AT2K, far).start()
+
+    def pass_on(number):
+        unit = ORDER[number]
+
         @pl.when(has_earlier)
         def _():
-            remote(half, h, 0, AT4, later).wait_recv()
+            landed(unit, AT4)
 
         @pl.when(jnp.logical_not(first))
         def _():
-            remote(half, h, 4, AT3, left).start()
+            remote(unit, BOTH, 4, 3, TO3, AT3, left).start()
 
         @pl.when(last)
         def _():
-            remote(half, h, 4, AT1, right).start()
-
-        @pl.when(jnp.logical_not(low))
-        def _():
-            remote(half, h, 4, AT2, far).start()
+            remote(unit, BOTH, 4, 1, TO1, AT1, right).start()
+            landed(unit, AT3)
+            remote(unit, VALUE, 3, 2, ON_LEFT, AT2V, left).start()
+
+        @pl.when(place == 2)
+        def _():
+            remote(unit, KEY, 4, 2, STRAIGHT, AT2K, far).start()
+
+        @pl.when((place == 1) | (place == 2))
+        def _():
+            landed(unit, AT1)
+
+            @pl.when(place == 1)
+            def _():
+                remote(unit, KEY, 1, 2, ON_RIGHT, AT2K, right).start()
+
+            @pl.when(place == 2)
+            def _():
+                remote(unit, VALUE, 1, 2, ON_RIGHT, AT2V, right).start()
+
+    def pass_far(number):
+        unit = ORDER[number]
+
+        @pl.when(first)
+        def _():
+            landed(unit, AT1)
+            remote(unit, KEY, 1, 2, ON_RIGHT, AT2K, right).start()
+
+        @pl.when((place == 1) | (place == 2))
+        def _():
+            landed(unit, AT3)
+            remote(unit, VALUE, 3, 2, ON_LEFT, AT2V, left).start()
 
     def project_kv(half, h):
         rows = own_rows if half == 0 else other_rows
@@ -247,13 +313,13 @@
             allowed = offset.astype(jnp.float32) + (base_f - float(slot * TOK)) >= start
             if slot == 0:
                 allowed = allowed & (offset <= row)
-            bias[:, pl.ds(slot * TOK + half * HEAD_SIZE, HEAD_SIZE)] = jnp.where(
+            bias[:, pl.ds(PLACE_OF[slot] * TOK + half * HEAD_SIZE, HEAD_SIZE)] = jnp.where(
                 allowed, 0.0, NEG_FILL
             )
 
     @pl.when(jnp.logical_not(has_earlier))
     def _():
-        kv[:, :, pl.ds(4 * TOK, TOK), :] = jnp.zeros((2, KV_HERE, TOK, HEAD_SIZE), jnp.bfloat16)
+        kv[:, :, pl.ds(PLACE_OF[4] * TOK, TOK), :] = jnp.zeros((2, KV_HERE, TOK, HEAD_SIZE), jnp.bfloat16)
 
     acc[...] = jnp.zeros_like(acc)
     x_exchange().wait()
@@ -268,26 +334,39 @@
         return carry
 
     lax.fori_loop(0, KV_HERE, project_other, 0)
-    pass_on(0, 0)
+    pass_on(0)
+    after_query = (
+        lambda: pass_on(1),
+        lambda: pass_on(2),
+        lambda: (pass_on(3), pass_far(0)),
+        lambda: (pass_on(4), pass_far(1)),
+    )
 
     def project_q(h, carry):
+        @pl.when(h < PLACES - KV_HERE)
+        def _():
+            start_all(wo_copies(h))
+
         wq_copy(h).wait()
-        wo_copy(h).start()
-        some = jnp.dot(x[...], wq[h], preferred_element_type=jnp.float32)
+        columns = weights[h].reshape(WIDTH, TILE)
+        some = jnp.dot(x[...], columns, preferred_element_type=jnp.float32)
         for number in range(GROUP):
             q[h * GROUP + number] = rotated(
                 some[:, number * HEAD_SIZE : (number + 1) * HEAD_SIZE], 2, slice(None)
             )
-        for step, (half, head_number) in enumerate(((0, 1), (1, 0), (1, 1), (0, 2))):
+
+        @pl.when(h < 2 * KV_HERE - PLACES)
+        def _():
+            start_all(wo_copies(h + PLACES - KV_HERE))
+
+        for step, actions in enumerate(after_query):
             @pl.when(h == step)
             def _():
-                pass_on(half, head_number)
+                actions()
 
         return carry
 
     lax.fori_loop(0, KV_HERE, project_q, 0)
-    pass_on(1, 2)
-
     def reduce_copy(chunk):
         return pltpu.make_async_remote_copy(
             src_ref=send.at[chunk],
@@ -298,53 +377,106 @@
             device_id_type=MESH,
         )
 
-    def attend(h, carry):
+    def values_of(h, rows):
+        values = kv[VALUE, h, rows, :]
+        return jnp.concatenate([values, jnp.ones_like(values)], axis=1)
+
+    def scores_of(h, number, rows):
+        score = lax.dot_general(
+            q[h * GROUP + number], kv[KEY, h, rows, :], (((1,), (1,)), ((), ())),
+            preferred_element_type=jnp.float32,
+        )
+        return score + bias[:, rows]
+
+    def attend_early(h):
         for half in range(2):
-            for slot in (AT1, AT2, AT3):
-                remote(half, h, 0, slot, far).wait_recv()
-        keys = kv[0, h, pl.ds(0, SLOTS * TOK), :]
-        values = kv[1, h, pl.ds(0, SLOTS * TOK), :]
-        values = jnp.concatenate([values, jnp.ones_like(values)], axis=1)
+            @pl.when(last)
+            def _():
+                landed((half, h), AT1)
+
+            @pl.when(first)
+            def _():
+                landed((half, h), AT3)
+
+        rows = slice(0, EARLY)
+        values = values_of(h, rows)
         for number in range(GROUP):
-            score = lax.dot_general(
-                q[h * GROUP + number], keys, (((1,), (1,)), ((), ())),
-                preferred_element_type=jnp.float32,
-            )
-            score = score + bias[...]
+            score = scores_of(h, number, rows)
             rowmax = jnp.max(score, axis=1, keepdims=True)
             weight = jnp.exp2(score - rowmax).astype(jnp.bfloat16)
-            mixed = jnp.dot(weight, values, preferred_element_type=jnp.float32)
+            kept = lax.rem(h, 2) * GROUP + number
+            partial[kept] = jnp.dot(weight, values, preferred_element_type=jnp.float32)
+            top[kept] = jnp.broadcast_to(rowmax, (TOK, HEAD_SIZE))
+
+    def attend_late(h):
+        for half in range(2):
+            landed((half, h), AT2K)
+            landed((half, h), AT2V)
+
+        rows = slice(EARLY, SLOTS * TOK)
+        values = values_of(h, rows)
+        for number in range(GROUP):
+            kept = lax.rem(h, 2) * GROUP + number
+            score = scores_of(h, number, rows)
+            before = top[kept]
+            rowmax = jnp.maximum(before, jnp.max(score, axis=1, keepdims=True))
+            factor = jnp.exp2(before - rowmax)
+            weight = jnp.exp2(score - jnp.concatenate([rowmax, rowmax], axis=1))
+            mixed = jnp.dot(weight.astype(jnp.bfloat16), values, preferred_element_type=jnp.float32)
+            mixed = mixed + partial[kept] * jnp.concatenate([factor, factor], axis=1)
             att[:, number * HEAD_SIZE : (number + 1) * HEAD_SIZE] = (
                 mixed[:, :HEAD_SIZE] / mixed[:, HEAD_SIZE:]
             ).astype(jnp.bfloat16)
 
-        @pl.when(h == 0)
-        def _():
-            pass_on(0, 3)
-            pass_on(1, 3)
-
-        wo_copy(h).wait()
-
-        def project_out(chunk, inner):
-            columns = lanes(chunk, WIDE_COLS)
-            acc[:, columns] += jnp.dot(
-                att[...], wo[h, :, columns], preferred_element_type=jnp.float32
-            )
-            return inner
-
-        @pl.when(h < KV_HERE - 1)
-        def _():
-            lax.fori_loop(0, WIDTH // WIDE_COLS, project_out, 0)
-
-        return carry
-
-    lax.fori_loop(0, KV_HERE, attend, 0)
+    def project_out(h):
+        wait_all(wo_copies(h))
+
+        def some(chunk, carry):
+            blocks = WIDE_COLS // TILE
+            for block, sums in enumerate(projected_out(h, chunk * blocks, blocks)):
+                acc[:, lanes(chunk * blocks + block, TILE)] += sums
+            return carry
+
+        lax.fori_loop(0, WIDTH // WIDE_COLS, some, 0)
+
+    def attend(step, carry):
+        def at(number, *actions):
+            @pl.when(step == number)
+            def _():
+                for action, unit in actions:
+                    action(unit)
+
+        at(0, (pass_on, 5), (pass_far, 2))
+        at(1, (pass_on, 6), (pass_far, 3))
+        at(2, (pass_far, 5))
+
+        @pl.when(step < KV_HERE)
+        def _():
+            attend_early(step)
+
+        at(1, (pass_on, 7), (pass_far, 4))
+        at(2, (pass_far, 6))
+
+        @pl.when(step >= 1)
+        def _():
+            attend_late(step - 1)
+
+        at(2, (pass_far, 7))
+
+        @pl.when((step >= 1) & (step < KV_HERE))
+        def _():
+            project_out(step - 1)
+
+        return carry
+
+    lax.fori_loop(0, KV_HERE + 1, attend, 0)
+    wait_all(wo_copies(KV_HERE - 1))
 
     def project_last(chunk, carry):
         columns = lanes(chunk, COLS)
-        acc[:, columns] += jnp.dot(
-            att[...], wo[KV_HERE - 1, :, columns], preferred_element_type=jnp.float32
-        )
+        blocks = COLS // TILE
+        for block, sums in enumerate(projected_out(KV_HERE - 1, chunk * blocks, blocks)):
+            acc[:, lanes(chunk * blocks + block, TILE)] += sums
         send[chunk] = acc[other_rows, columns].astype(jnp.bfloat16)
         reduce_copy(chunk).start()
         return carry
@@ -363,12 +495,27 @@
 
     def sent(h, carry):
         for half in range(2):
+            def gone(parts, leaving):
+                remote((half, h), parts, 0, 0, leaving, AT4, right).wait_send()
+
+            gone(BOTH, TO1)
+            gone(BOTH, TO3)
+
             @pl.when(has_later)
             def _():
-                remote(half, h, 0, AT4, later).wait_send()
-
-            for slot in (AT1, AT2, AT3):
-                remote(half, h, 0, slot, far).wait_send()
+                gone(BOTH, TO4)
+
+            @pl.when((place == 1) | (place == 2))
+            def _():
+                gone(KEY, STRAIGHT)
+
+            @pl.when(jnp.logical_not(last))
+            def _():
+                gone(KEY, ON_RIGHT)
+
+            @pl.when(jnp.logical_not(first))
+            def _():
+                gone(VALUE, ON_LEFT)
 
         return carry
 
@@ -388,8 +535,7 @@
         scratch_shapes=[
             pltpu.VMEM((TOK, WIDTH), jnp.bfloat16),
             pltpu.VMEM((KV_HERE, WIDTH, 2 * HEAD_SIZE), jnp.bfloat16),
-            pltpu.VMEM((KV_HERE, WIDTH, wide), jnp.bfloat16),
-            pltpu.VMEM((KV_HERE, wide, WIDTH), jnp.bfloat16),
+            pltpu.VMEM((PLACES, WIDTH // TILE, TILE, TILE), jnp.bfloat16),
             pltpu.VMEM((KV_HERE * GROUP, TOK, HEAD_SIZE), jnp.bfloat16),
             pltpu.VMEM((2, KV_HERE, SLOTS * TOK, HEAD_SIZE), jnp.bfloat16),
             pltpu.VMEM((TOK, WIDTH), jnp.float32),
@@ -399,14 +545,16 @@
             pltpu.VMEM((TOK, SLOTS * TOK), jnp.float32),
             pltpu.VMEM((2 * TOK + 2 * N_SEQ, HEAD_SIZE), jnp.float32),
             pltpu.VMEM((4, TOK, HEAD_SIZE), jnp.float32),
-            dma(()), dma((KV_HERE, 2)), dma((KV_HERE,)), dma((KV_HERE,)), dma(()),
-            dma(()), dma(()), dma((UNITS, SLOTS)), dma((UNITS, SLOTS)), dma((CHUNKS,)), dma((CHUNKS,)),
+            pltpu.VMEM((2 * GROUP, TOK, 2 * HEAD_SIZE), jnp.float32),
+            pltpu.VMEM((2 * GROUP, TOK, HEAD_SIZE), jnp.float32),
+            dma(()), dma((KV_HERE, 2)), dma((KV_HERE,)), dma((KV_HERE, WIDTH // TILE)), dma(()),
+            dma(()), dma(()), dma((UNITS, 6)), dma((UNITS, 5)), dma((CHUNKS,)), dma((CHUNKS,)),
         ],
         compiler_params=pltpu.CompilerParams(
-            collective_id=0, has_side_effects=True, vmem_limit_bytes=62 << 20
+            collective_id=0, has_side_effects=True, vmem_limit_bytes=52 << 20
         ),
         name="layer",
-    )(input_rows, doc_lengths, w_query, key_weight, value_weight, w_out, table)
+    )(input_rows, doc_lengths, w_query.reshape(WIDTH // TILE, TILE, -1), key_weight, value_weight, w_out, table)
 
 
 def solution(mesh):

time: 50.6 us -> 46.8 us (0.925); the launches traced: 50.5 us -> 46 us
  Pallas kernels: 48.2 us -> 43.4 us
    pallas_call x1, Pallas kernels: 48.2 us -> 43.4 us  [body(): pl.pallas_call(kernel, out_shape=jax.ShapeDtypeStruct((HALF, WIDTH), jnp....]
    unnamed x1 -> x5, local copies, waits for them, and re-layouts: 2.29 us -> 2.62 us
where the time goes in v4:
time: 46.8 us; the launch traced here: 46 us
  Pallas kernels  43.4 us (93%)
  local copies, waits for them, and re-layouts  2.62 us (6%)
    pallas_call x1, Pallas kernels, body(): pl.pallas_call(kernel, out_shape=jax.ShapeDtypeStruct((HALF, WIDTH), jnp....  43.4 us
    unnamed x5, local copies, waits for them, and re-layouts  2.62 us

profile of v4, /device:TPU:225, one launch (start us, length us, event | category | flops | bytes accessed | tf_op | source)
XLA Modules:
  0.0 46.0 jit_solution(11137386728642699061)
XLA Ops:
  0.0 0.0 copy-start
  0.0 1.0 %copy-done = f32[768,128]{1,0:T(8,128)S(1)} copy-done((f32[768,128]{1,0:T(8,128)S(1)}, f32[768,128]{1,0:T(8,128)}, u32[]{:S(2)}) %copy-start) | copy-done | bytes 393240
  1.0 0.0 copy-start.1
  1.0 0.7 %copy-done.1 = s32[64]{0:T(128)S(1)} copy-done((s32[64]{0:T(128)S(1)}, s32[64]{0:T(128)}, u32[]{:S(2)}) %copy-start.1) | copy-done | bytes 280
  1.7 43.4 %layer.1 = bf16[128,4096]{1,0:T(8,128)(2,1)S(1)} custom-call(bf16[128,4096]{1,0:T(8,128)(2,1)} %x_hbm.1, s32[64]{0:T(128)S(1)} %copy-done.1, bf16[8,512,2048]{2,1,0:T(8,128)(2,1)} %bitcast.1, bf16[4096,512]{1,0:T(8,128)(2,1)} %wk_hbm.1, bf16[4096,512]{1,0:T(8,128)(2,1)} %wv_hbm.1, bf16[2048,4096]{1,0:T(8,128)(2,1)} %wo_hbm.1, f32[768,128]{1,0:T(8,128)S(1)} %copy-done), custom_call_target="tpu_custom_call" | custom-call | tf_op jit(solution)/shard_map/layer/pallas_call | solution.py:530
  45.0 1.0 %copy.9 = bf16[128,4096]{1,0:T(8,128)(2,1)} copy(bf16[128,4096]{1,0:T(8,128)(2,1)S(1)} %layer.1) | data formatting | bytes 2097152
Async XLA Ops:
  0.0 1.0 %copy-start = (f32[768,128]{1,0:T(8,128)S(1)}, f32[768,128]{1,0:T(8,128)}, u32[]{:S(2)}) copy-start(f32[768,128]{1,0:T(8,128)} %constant.2.clone.tab_hbm) | copy-start | bytes 1179652
  1.0 0.7 %copy-start.1 = (s32[64]{0:T(128)S(1)}, s32[64]{0:T(128)}, u32[]{:S(2)}) copy-start(s32[64]{0:T(128)} %docs.1) | copy-start | bytes 772

commit v5 on v4

--- a/solution.py
+++ b/solution.py
@@ -50,13 +50,17 @@
     return np.asarray(table, dtype=np.float32).astype(np.float64)
 
 
+SUBLANES = 8
+SCORE_SCALE = HEAD_SIZE ** (-0.5) * math.log2(math.e)
+
+
 def rotary_tables():
     freq = np.concatenate([inverse_frequency()] * 2)
     rows = np.arange(TOK)[:, None] * freq
-    starts = (np.arange(N_SEQ) * TOK)[:, None] * freq
-    return np.concatenate(
-        [np.cos(rows), np.sin(rows), np.cos(starts), np.sin(starts)]
-    ).astype(np.float32)
+    starts = np.repeat(np.arange(N_SEQ) * TOK, SUBLANES)[:, None] * freq
+    offsets = [np.cos(rows), np.sin(rows)]
+    scaled = [SCORE_SCALE * table for table in offsets]
+    return np.concatenate(offsets + scaled + [np.cos(starts), np.sin(starts)]).astype(np.float32)
 
 
 def kernel(
@@ -84,7 +88,19 @@
     other_rows = pl.ds(pl.multiple_of(other * HALF, HALF), HALF)
 
     x_copy = pltpu.make_async_copy(x_hbm, x.at[own_rows, :], x_sem)
-    tab_copy = pltpu.make_async_copy(tab_hbm, tab, tab_sem)
+    starts_at = 4 * TOK
+    tab_copies = [
+        pltpu.make_async_copy(
+            tab_hbm.at[pl.ds(pl.multiple_of(source, SUBLANES), rows), :], tab.at[pl.ds(target, rows), :], tab_sem.at[number]
+        )
+        for number, (source, target, rows) in enumerate(
+            (
+                (0, 0, starts_at),
+                (starts_at + seq * SUBLANES, starts_at, SUBLANES),
+                (starts_at + (N_SEQ + seq) * SUBLANES, starts_at + SUBLANES, SUBLANES),
+            )
+        )
+    ]
 
     def lanes(number, size):
         return pl.ds(pl.multiple_of(number * size, size), size)
@@ -134,7 +150,8 @@
         ]
 
     x_copy.start()
-    tab_copy.start()
+    for copy in tab_copies:
+        copy.start()
     for h in range(KV_HERE):
         for copy in wkv_copies(h):
             copy.start()
@@ -168,18 +185,15 @@
     lane = lax.broadcasted_iota(jnp.int32, (TOK, HEAD_SIZE), 1)
     row = lax.broadcasted_iota(jnp.int32, (TOK, HEAD_SIZE), 0)
 
-    tab_copy.wait()
-    cos_row, sin_row = tab[pl.ds(0, TOK), :], tab[pl.ds(TOK, TOK), :]
-    cos_base = tab[pl.ds(2 * TOK + seq, 1), :]
-    sin_base = tab[pl.ds(2 * TOK + N_SEQ + seq, 1), :]
-    cosine = cos_row * cos_base - sin_row * sin_base
-    sine = sin_row * cos_base + cos_row * sin_base
-    sine = jnp.where(lane < HEAD_SIZE // 2, -sine, sine)
-    scale = HEAD_SIZE ** (-0.5) * math.log2(math.e)
-    rope[0] = cosine
-    rope[1] = sine
-    rope[2] = cosine * scale
-    rope[3] = sine * scale
+    for copy in tab_copies:
+        copy.wait()
+    cos_base = tab[pl.ds(starts_at, 1), :]
+    sin_base = tab[pl.ds(starts_at + SUBLANES, 1), :]
+    for which in (0, 2):
+        cos_row, sin_row = tab[pl.ds(which * TOK, TOK), :], tab[pl.ds((which + 1) * TOK, TOK), :]
+        sine = sin_row * cos_base + cos_row * sin_base
+        rope[which] = cos_row * cos_base - sin_row * sin_base
+        rope[which + 1] = jnp.where(lane < HEAD_SIZE // 2, -sine, sine)
 
     def rotated(value, which, rows):
         turned = pltpu.roll(value, HEAD_SIZE // 2, 1)
@@ -238,13 +252,17 @@
         @pl.when(last)
         def _():
             remote(unit, BOTH, 4, 1, TO1, AT1, right).start()
+
+        @pl.when(place == 2)
+        def _():
+            remote(unit, KEY, 4, 2, STRAIGHT, AT2K, far).start()
+
+    def pass_own_row(unit):
+        @pl.when(last)
+        def _():
             landed(unit, AT3)
             remote(unit, VALUE, 3, 2, ON_LEFT, AT2V, left).start()
 
-        @pl.when(place == 2)
-        def _():
-            remote(unit, KEY, 4, 2, STRAIGHT, AT2K, far).start()
-
         @pl.when((place == 1) | (place == 2))
         def _():
             landed(unit, AT1)
@@ -269,6 +287,8 @@
         def _():
             landed(unit, AT3)
             remote(unit, VALUE, 3, 2, ON_LEFT, AT2V, left).start()
+
+        pass_own_row(unit)
 
     def project_kv(half, h):
         rows = own_rows if half == 0 else other_rows
@@ -543,15 +563,15 @@
             pltpu.VMEM((CHUNKS, HALF, COLS), jnp.bfloat16),
             pltpu.VMEM((TOK, wide), jnp.bfloat16),
             pltpu.VMEM((TOK, SLOTS * TOK), jnp.float32),
-            pltpu.VMEM((2 * TOK + 2 * N_SEQ, HEAD_SIZE), jnp.float32),
+            pltpu.VMEM((4 * TOK + 2 * SUBLANES, HEAD_SIZE), jnp.float32),
             pltpu.VMEM((4, TOK, HEAD_SIZE), jnp.float32),
             pltpu.VMEM((2 * GROUP, TOK, 2 * HEAD_SIZE), jnp.float32),
             pltpu.VMEM((2 * GROUP, TOK, HEAD_SIZE), jnp.float32),
-            dma(()), dma((KV_HERE, 2)), dma((KV_HERE,)), dma((KV_HERE, WIDTH // TILE)), dma(()),
+            dma(()), dma((KV_HERE, 2)), dma((KV_HERE,)), dma((KV_HERE, WIDTH // TILE)), dma((3,)),
             dma(()), dma(()), dma((UNITS, 6)), dma((UNITS, 5)), dma((CHUNKS,)), dma((CHUNKS,)),
         ],
         compiler_params=pltpu.CompilerParams(
-            collective_id=0, has_side_effects=True, vmem_limit_bytes=52 << 20
+            collective_id=0, has_side_effects=True, vmem_limit_bytes=(52 << 20) + (1 << 19)
         ),
         name="layer",
     )(input_rows, doc_lengths, w_query.reshape(WIDTH // TILE, TILE, -1), key_weight, value_weight, w_out, table)

time: 46.8 us -> 45.5 us (0.972); the launches traced: 46 us -> 45.4 us
  local copies, waits for them, and re-layouts: 2.62 us -> 1.63 us
    unnamed x5 -> x3, local copies, waits for them, and re-layouts: 2.62 us -> 1.63 us
where the time goes in v5:
time: 45.5 us; the launch traced here: 45.4 us
  Pallas kernels  43.8 us (96%)
  local copies, waits for them, and re-layouts  1.63 us (4%)
    pallas_call x1, Pallas kernels, body(): pl.pallas_call(kernel, out_shape=jax.ShapeDtypeStruct((HALF, WIDTH), jnp....  43.8 us
    unnamed x3, local copies, waits for them, and re-layouts  1.63 us

profile of v5, /device:TPU:225, one launch (start us, length us, event | category | flops | bytes accessed | tf_op | source)
XLA Modules:
  0.0 45.4 jit_solution(2049108471503044901)
XLA Ops:
  0.0 0.0 copy-start
  0.0 0.7 %copy-done = s32[64]{0:T(128)S(1)} copy-done((s32[64]{0:T(128)S(1)}, s32[64]{0:T(128)}, u32[]{:S(2)}) %copy-start) | copy-done | bytes 280
  0.7 43.8 %layer.1 = bf16[128,4096]{1,0:T(8,128)(2,1)S(1)} custom-call(bf16[128,4096]{1,0:T(8,128)(2,1)} %x_hbm.1, s32[64]{0:T(128)S(1)} %copy-done, bf16[8,512,2048]{2,1,0:T(8,128)(2,1)} %bitcast.1, bf16[4096,512]{1,0:T(8,128)(2,1)} %wk_hbm.1, bf16[4096,512]{1,0:T(8,128)(2,1)} %wv_hbm.1, bf16[2048,4096]{1,0:T(8,128)(2,1)} %wo_hbm.1, f32[3072,128]{1,0:T(8,128)} %constant.2.clone.tab_hbm), custom_call_target="tpu_custom_call" | custom-call | tf_op jit(solution)/shard_map/layer/pallas_call | solution.py:550
  44.5 1.0 %copy.9 = bf16[128,4096]{1,0:T(8,128)(2,1)} copy(bf16[128,4096]{1,0:T(8,128)(2,1)S(1)} %layer.1) | data formatting | bytes 2097152
Async XLA Ops:
  0.0 0.7 %copy-start = (s32[64]{0:T(128)S(1)}, s32[64]{0:T(128)}, u32[]{:S(2)}) copy-start(s32[64]{0:T(128)} %docs.1) | copy-start | bytes 772

commit v6 on v4

--- a/solution.py
+++ b/solution.py
@@ -238,13 +238,17 @@
         @pl.when(last)
         def _():
             remote(unit, BOTH, 4, 1, TO1, AT1, right).start()
+
+        @pl.when(place == 2)
+        def _():
+            remote(unit, KEY, 4, 2, STRAIGHT, AT2K, far).start()
+
+    def pass_own_row(unit):
+        @pl.when(last)
+        def _():
             landed(unit, AT3)
             remote(unit, VALUE, 3, 2, ON_LEFT, AT2V, left).start()
 
-        @pl.when(place == 2)
-        def _():
-            remote(unit, KEY, 4, 2, STRAIGHT, AT2K, far).start()
-
         @pl.when((place == 1) | (place == 2))
         def _():
             landed(unit, AT1)
@@ -269,6 +273,8 @@
         def _():
             landed(unit, AT3)
             remote(unit, VALUE, 3, 2, ON_LEFT, AT2V, left).start()
+
+        pass_own_row(unit)
 
     def project_kv(half, h):
         rows = own_rows if half == 0 else other_rows

time: 46.8 us -> 44.6 us (0.953); the launches traced: 46 us -> 44.4 us
  Pallas kernels: 43.4 us -> 41.8 us
    pallas_call x1, Pallas kernels: 43.4 us -> 41.8 us  [body(): pl.pallas_call(kernel, out_shape=jax.ShapeDtypeStruct((HALF, WIDTH), jnp....]
where the time goes in v6:
time: 44.6 us; the launch traced here: 44.4 us
  Pallas kernels  41.8 us (94%)
  local copies, waits for them, and re-layouts  2.62 us (6%)
    pallas_call x1, Pallas kernels, body(): pl.pallas_call(kernel, out_shape=jax.ShapeDtypeStruct((HALF, WIDTH), jnp....  41.8 us
    unnamed x5, local copies, waits for them, and re-layouts  2.62 us

profile of v6, /device:TPU:225, one launch (start us, length us, event | category | flops | bytes accessed | tf_op | source)
XLA Modules:
  0.0 44.4 jit_solution(1514713295384929827)
XLA Ops:
  0.0 0.0 copy-start
  0.0 1.0 %copy-done = f32[768,128]{1,0:T(8,128)S(1)} copy-done((f32[768,128]{1,0:T(8,128)S(1)}, f32[768,128]{1,0:T(8,128)}, u32[]{:S(2)}) %copy-start) | copy-done | bytes 393240
  1.0 0.0 copy-start.1
  1.0 0.7 %copy-done.1 = s32[64]{0:T(128)S(1)} copy-done((s32[64]{0:T(128)S(1)}, s32[64]{0:T(128)}, u32[]{:S(2)}) %copy-start.1) | copy-done | bytes 280
  1.7 41.8 %layer.1 = bf16[128,4096]{1,0:T(8,128)(2,1)S(1)} custom-call(bf16[128,4096]{1,0:T(8,128)(2,1)} %x_hbm.1, s32[64]{0:T(128)S(1)} %copy-done.1, bf16[8,512,2048]{2,1,0:T(8,128)(2,1)} %bitcast.1, bf16[4096,512]{1,0:T(8,128)(2,1)} %wk_hbm.1, bf16[4096,512]{1,0:T(8,128)(2,1)} %wv_hbm.1, bf16[2048,4096]{1,0:T(8,128)(2,1)} %wo_hbm.1, f32[768,128]{1,0:T(8,128)S(1)} %copy-done), custom_call_target="tpu_custom_call" | custom-call | tf_op jit(solution)/shard_map/layer/pallas_call | solution.py:536
  43.5 1.0 %copy.9 = bf16[128,4096]{1,0:T(8,128)(2,1)} copy(bf16[128,4096]{1,0:T(8,128)(2,1)S(1)} %layer.1) | data formatting | bytes 2097152
Async XLA Ops:
  0.0 1.0 %copy-start = (f32[768,128]{1,0:T(8,128)S(1)}, f32[768,128]{1,0:T(8,128)}, u32[]{:S(2)}) copy-start(f32[768,128]{1,0:T(8,128)} %constant.2.clone.tab_hbm) | copy-start | bytes 1179652
  1.0 0.7 %copy-start.1 = (s32[64]{0:T(128)S(1)}, s32[64]{0:T(128)}, u32[]{:S(2)}) copy-start(s32[64]{0:T(128)} %docs.1) | copy-start | bytes 772

commit v7 on v6

--- a/solution.py
+++ b/solution.py
@@ -489,6 +489,34 @@
 
     lax.fori_loop(0, CHUNKS, project_last, 0)
 
+    def sent(h, carry):
+        for half in range(2):
+            def gone(parts, leaving):
+                remote((half, h), parts, 0, 0, leaving, AT4, right).wait_send()
+
+            gone(BOTH, TO1)
+            gone(BOTH, TO3)
+
+            @pl.when(has_later)
+            def _():
+                gone(BOTH, TO4)
+
+            @pl.when((place == 1) | (place == 2))
+            def _():
+                gone(KEY, STRAIGHT)
+
+            @pl.when(jnp.logical_not(last))
+            def _():
+                gone(KEY, ON_RIGHT)
+
+            @pl.when(jnp.logical_not(first))
+            def _():
+                gone(VALUE, ON_LEFT)
+
+        return carry
+
+    lax.fori_loop(0, KV_HERE, sent, 0)
+
     def finish(chunk, carry):
         columns = lanes(chunk, COLS)
         reduce_copy(chunk).wait()
@@ -498,34 +526,6 @@
         return carry
 
     lax.fori_loop(0, CHUNKS, finish, 0)
-
-    def sent(h, carry):
-        for half in range(2):
-            def gone(parts, leaving):
-                remote((half, h), parts, 0, 0, leaving, AT4, right).wait_send()
-
-            gone(BOTH, TO1)
-            gone(BOTH, TO3)
-
-            @pl.when(has_later)
-            def _():
-                gone(BOTH, TO4)
-
-            @pl.when((place == 1) | (place == 2))
-            def _():
-                gone(KEY, STRAIGHT)
-
-            @pl.when(jnp.logical_not(last))
-            def _():
-                gone(KEY, ON_RIGHT)
-
-            @pl.when(jnp.logical_not(first))
-            def _():
-                gone(VALUE, ON_LEFT)
-
-        return carry
-
-    lax.fori_loop(0, KV_HERE, sent, 0)
 
 
 def body(input_rows, doc_lengths, w_query, key_weight, value_weight, w_out):

time: 44.6 us -> 44.5 us (level)
  no operation moved by 1% of the time
where the time goes in v7:
time: 44.5 us; the launch traced here: 44.3 us
  Pallas kernels  41.7 us (94%)
  local copies, waits for them, and re-layouts  2.62 us (6%)
    pallas_call x1, Pallas kernels, body(): pl.pallas_call(kernel, out_shape=jax.ShapeDtypeStruct((HALF, WIDTH), jnp....  41.7 us
    unnamed x5, local copies, waits for them, and re-layouts  2.62 us

profile of v7, /device:TPU:225, one launch (start us, length us, event | category | flops | bytes accessed | tf_op | source)
XLA Modules:
  0.0 44.3 jit_solution(12711984013422678197)
XLA Ops:
  0.0 0.0 copy-start
  0.0 1.0 %copy-done = f32[768,128]{1,0:T(8,128)S(1)} copy-done((f32[768,128]{1,0:T(8,128)S(1)}, f32[768,128]{1,0:T(8,128)}, u32[]{:S(2)}) %copy-start) | copy-done | bytes 393240
  1.0 0.0 copy-start.1
  1.0 0.7 %copy-done.1 = s32[64]{0:T(128)S(1)} copy-done((s32[64]{0:T(128)S(1)}, s32[64]{0:T(128)}, u32[]{:S(2)}) %copy-start.1) | copy-done | bytes 280
  1.7 41.7 %layer.1 = bf16[128,4096]{1,0:T(8,128)(2,1)S(1)} custom-call(bf16[128,4096]{1,0:T(8,128)(2,1)} %x_hbm.1, s32[64]{0:T(128)S(1)} %copy-done.1, bf16[8,512,2048]{2,1,0:T(8,128)(2,1)} %bitcast.1, bf16[4096,512]{1,0:T(8,128)(2,1)} %wk_hbm.1, bf16[4096,512]{1,0:T(8,128)(2,1)} %wv_hbm.1, bf16[2048,4096]{1,0:T(8,128)(2,1)} %wo_hbm.1, f32[768,128]{1,0:T(8,128)S(1)} %copy-done), custom_call_target="tpu_custom_call" | custom-call | tf_op jit(solution)/shard_map/layer/pallas_call | solution.py:536
  43.4 1.0 %copy.9 = bf16[128,4096]{1,0:T(8,128)(2,1)} copy(bf16[128,4096]{1,0:T(8,128)(2,1)S(1)} %layer.1) | data formatting | bytes 2097152
Async XLA Ops:
  0.0 1.0 %copy-start = (f32[768,128]{1,0:T(8,128)S(1)}, f32[768,128]{1,0:T(8,128)}, u32[]{:S(2)}) copy-start(f32[768,128]{1,0:T(8,128)} %constant.2.clone.tab_hbm) | copy-start | bytes 1179652
  1.0 0.7 %copy-start.1 = (s32[64]{0:T(128)S(1)}, s32[64]{0:T(128)}, u32[]{:S(2)}) copy-start(s32[64]{0:T(128)} %docs.1) | copy-start | bytes 772
